TPU v7x, 128 devices: a whole 4x4x4 slice. The times are simulated.
128 devices in a mesh: tx: 16 (over y, x), ty: 8 (over z, core).
Axes of the slice: x: 4, y: 4, z: 4, core: 2. Of those that a mesh axis runs over, the one named last changes fastest.
Arguments:
- adjoint_in: float32 [50, 1024, 1024], P(None, 'tx', 'ty'), may hold values from -6 to 6
- state_theta: bfloat16 [50, 1024, 1024], P(None, 'tx', 'ty'), may hold values from -6 to 6
- state_u: bfloat16 [50, 1024, 1024], P(None, 'tx', 'ty'), may hold values from -1.796875 to 1.796875
- state_v: bfloat16 [50, 1024, 1024], P(None, 'tx', 'ty'), may hold values from -1.796875 to 1.796875
- level_scale: float32 [3, 50], replicated, may hold values from 0.5 to 2
- land_mask: int32 [1024, 1024], P('tx', 'ty'), may hold values 0 or 1
- level_weights: float32 [50], replicated, may hold values from 0.02 to 0.2
- column_weight: float32 [1024, 1024], P('tx', 'ty'), may hold values from 0.5 to 2
Outputs:
- adjoint_out: float32 [50, 1024, 1024], P(None, 'tx', 'ty')
- surface_adjoint: float32 [1024, 1024], P('tx', 'ty')
All inputs are finite; a program needn't handle non-finite values. No bound on the sum of `land_mask` on one device may be relied on, other than what follows from the above.
Results may differ from a plain program's by a relative error of at most 0.0003.
Values may be sent and summed in bfloat16 or wider, within the bound.
No kernel may reach another device: no remote copies, remote signals or barrier semaphores. Data moves between devices by JAX's collectives and lax.ppermute only.
A program may use at most 192 MiB of HBM per device.

v0:
```python
import jax
import jax.numpy as jnp
from jax import lax
from jax.sharding import PartitionSpec as P

ITERS = 12


def extended(value, sides, width):
    for axis, dim in sides:
        size, length = (lax.axis_size(axis), value.shape[dim])
        up = [(i, (i + 1) % size) for i in range(size - 1)]
        down = [(j, i) for i, j in up]
        last = lax.slice_in_dim(value, length - width, length, axis=dim)
        initial = lax.slice_in_dim(value, 0, width, axis=dim)
        before = lax.ppermute(last, axis, up)
        after = lax.ppermute(initial, axis, down)
        value = jnp.concatenate([before, value, after], axis=dim)
    return value


def interior(p):
    return p[..., 1:-1, 1:-1]


def stepped_field(lam, theta, vel_u, vel_v, wet):
    kappa = 0.05 * (1.5 + jnp.tanh(theta))
    lc = interior(lam)
    le = lam[..., 2:, 1:-1]
    lw = lam[..., :-2, 1:-1]
    ln = lam[..., 1:-1, 2:]
    ls = lam[..., 1:-1, :-2]
    kc = interior(kappa)
    mc = interior(wet)
    m_east = mc * wet[2:, 1:-1]
    m_west = mc * wet[:-2, 1:-1]
    m_north = mc * wet[1:-1, 2:]
    m_south = mc * wet[1:-1, :-2]
    diffusion = 0.5 * (kc + kappa[..., 2:, 1:-1]) * m_east * (le - lc)
    diffusion = diffusion - 0.5 * (kc + kappa[..., :-2, 1:-1]) * m_west * (lc - lw)
    diffusion = diffusion + 0.5 * (kc + kappa[..., 1:-1, 2:]) * m_north * (ln - lc)
    diffusion = diffusion - 0.5 * (kc + kappa[..., 1:-1, :-2]) * m_south * (lc - ls)
    advection = m_east * interior(vel_u) * 0.5 * (le - lc) + m_west * vel_u[
        ..., :-2, 1:-1
    ] * 0.5 * (lc - lw)
    advection = (
        advection
        + m_north * interior(vel_v) * 0.5 * (ln - lc)
        + m_south * vel_v[..., 1:-1, :-2] * 0.5 * (lc - ls)
    )
    kface = 0.5 * (kc[1:] + kc[:-1])
    zflux = kface * (lc[1:] - lc[:-1])
    zeros = jnp.zeros_like(lc[:1])
    vertical = jnp.concatenate([zflux, zeros], 0) - jnp.concatenate([zeros, zflux], 0)
    return mc * (lc + diffusion + vertical + advection)


def apply_surface(padded, wet, column_weight):
    mc = interior(wet)
    sc = interior(padded)
    total = mc * wet[2:, 1:-1] * (sc - padded[2:, 1:-1])
    total = total + mc * wet[:-2, 1:-1] * (sc - padded[:-2, 1:-1])
    total = total + mc * wet[1:-1, 2:] * (sc - padded[1:-1, 2:])
    total = total + mc * wet[1:-1, :-2] * (sc - padded[1:-1, :-2])
    return column_weight * sc + 4.0 * total


def surface_operator(field, wet, column_weight):
    padded = extended(field, (("tx", 0), ("ty", 1)), 1)
    return apply_surface(padded, wet, column_weight)


def squares_total(residual):
    return lax.psum(jnp.sum(residual * residual), ("tx", "ty"))


def on_device(
    adjoint_in, state_theta, state_u, state_v, level_scale, land_mask, level_weights, column_weight
):
    levels = adjoint_in.shape[0]
    theta_scale = level_scale[0][:, None, None]
    u_scale = level_scale[1][:, None, None]
    v_scale = level_scale[2][:, None, None]
    packed = jnp.concatenate(
        [state_theta, state_u, state_v, land_mask.astype(jnp.bfloat16)[None]], 0
    )
    widened = extended(packed, (("tx", 1), ("ty", 2)), 1)
    lam = extended(adjoint_in, (("tx", 1), ("ty", 2)), 1)
    theta = widened[:levels].astype(jnp.float32) * theta_scale
    vel_u = widened[levels : 2 * levels].astype(jnp.float32) * u_scale
    vel_v = widened[2 * levels : 3 * levels].astype(jnp.float32) * v_scale
    wet = widened[3 * levels].astype(jnp.float32)
    stepped = stepped_field(lam, theta, vel_u, vel_v, wet)
    rhs = jnp.sum(level_weights[:, None, None] * stepped, axis=0)
    wet_inner = land_mask.astype(jnp.float32)
    surface = jnp.zeros_like(rhs)
    residual = rhs
    direction = rhs
    norm_now = squares_total(residual)
    for step in range(ITERS):
        image = surface_operator(direction, wet, column_weight)
        alpha = norm_now / lax.psum(jnp.sum(direction * image), ("tx", "ty"))
        surface = surface + alpha * direction
        residual = residual - alpha * image
        norm_next = squares_total(residual)
        direction = residual + norm_next / norm_now * direction
        norm_now = norm_next
    adjoint_out = stepped - level_weights[:, None, None] * (wet_inner * surface)[None]
    return (adjoint_out, surface)


def solution(mesh):
    placed = (
        P(None, "tx", "ty"),
        P(None, "tx", "ty"),
        P(None, "tx", "ty"),
        P(None, "tx", "ty"),
        P(),
        P("tx", "ty"),
        P(),
        P("tx", "ty"),
    )
    return jax.shard_map(
        on_device,
        mesh=mesh,
        in_specs=placed,
        out_specs=(P(None, "tx", "ty"), P("tx", "ty")),
        check_vma=False,
    )
```

profile of v0, /device:TPU:1, one launch (start us, length us, event | category | flops | bytes accessed | tf_op | source)
XLA Modules:
  0.0 1884.8 jit_solution(10013341342031551691)
XLA Ops:
  9.9 6.2 fusion.203
  16.1 4.0 copy.84
  24.1 4.0 copy.85
  31.8 5.2 collective-permute-start.5
  55.4 4.9 collective-permute-start.2
  70.6 26.7 %pad_maximum_fusion = bf16[151,66,130]{1,2,0:T(8,128)(2,1)S(1)} fusion(bf16[151,66,1]{1,2,0:T(2,128)(2,1)S(1)} %copy.91, bf16[151,1,128]{1,2,0:T(8,128)(2,1)} %copy.87, bf16[1,64,128]{1,2,0:T(8,128)(2,1)S(1)} %copy.83, bf16[50,64,128]{1,2,0:T(8,128)(2,1)} %copy.82, bf16[50,64,128]{1,2,0:T(8,128)(2,1)} %copy.81, bf16[50,64,128]{1,2,0:T(8,128)(2,1)} %copy-done.2, ...), kind=kLoop, calls=%fused_computation | loop fusion | flops 20729280 | bytes 5182320 | tf_op jit(solution)/shard_map/concatenate | solution.py:18
  105.1 32.4 %multiply_reduce_fusion = (f32[64,128]{0,1:T(8,128)}, f32[50,64,128]{1,2,0:T(8,128)}) fusion(f32[50]{0:T(128)S(1)} %copy-done.22, f32[50,66,130]{1,2,0:T(8,128)} %get-tuple-element.68, f32[64,128]{0,1:T(8,128)} %get-tuple-element.101, f32[64,128]{0,1:T(8,128)} %get-tuple-element.103, f32[50,66,130]{1,2,0:T(8,128)} %get-tuple-element.69, ...), kind=kLoop, calls=%fused_computation.52 | loop fusion | flops 20062208 | bytes 20033512 | tf_op jit(solution)/shard_map/reduce_sum | solution.py:94
  154.8 73.4 %all-reduce.2 = (f32[]{:T(128)}, f32[]{:T(128)}) all-reduce(f32[]{:T(128)} %get-tuple-element.9, f32[]{:T(128)} %get-tuple-element.8), channel_id=1, replica_groups=mesh['tx'=16,'ty'=8] {'tx','ty'}, use_global_device_ids=true, to_apply=%region_2.0 | all-reduce | flops 2 | bytes 16 | tf_op jit(solution)/shard_map/psum | solution.py:74
  230.9 62.8 %psum.170 = f32[]{:T(128)} all-reduce(f32[]{:T(128)} %multiply_reduce_fusion.21), channel_id=1, replica_groups=mesh['tx'=16,'ty'=8] {'tx','ty'}, use_global_device_ids=true, to_apply=%region_6.0 | all-reduce | flops 1 | bytes 8 | tf_op jit(solution)/shard_map/psum | solution.py:74
  311.7 66.9 %psum.171 = f32[]{:T(128)} all-reduce(f32[]{:T(128)} %get-tuple-element.50), channel_id=1, replica_groups=mesh['tx'=16,'ty'=8] {'tx','ty'}, use_global_device_ids=true, to_apply=%region_8.0 | all-reduce | flops 1 | bytes 8 | tf_op jit(solution)/shard_map/psum | solution.py:102
  381.5 63.0 %psum.172 = f32[]{:T(128)} all-reduce(f32[]{:T(128)} %get-tuple-element.48), channel_id=1, replica_groups=mesh['tx'=16,'ty'=8] {'tx','ty'}, use_global_device_ids=true, to_apply=%region_10.0 | all-reduce | flops 1 | bytes 8 | tf_op jit(solution)/shard_map/psum | solution.py:74
  447.2 4.0 collective-permute-start.17
  460.1 68.1 %psum.173 = f32[]{:T(128)} all-reduce(f32[]{:T(128)} %get-tuple-element.46), channel_id=1, replica_groups=mesh['tx'=16,'ty'=8] {'tx','ty'}, use_global_device_ids=true, to_apply=%region_12.0 | all-reduce | flops 1 | bytes 8 | tf_op jit(solution)/shard_map/psum | solution.py:102
  530.2 62.6 %psum.174 = f32[]{:T(128)} all-reduce(f32[]{:T(128)} %get-tuple-element.44), channel_id=1, replica_groups=mesh['tx'=16,'ty'=8] {'tx','ty'}, use_global_device_ids=true, to_apply=%region_14.0 | all-reduce | flops 1 | bytes 8 | tf_op jit(solution)/shard_map/psum | solution.py:74
  595.5 4.0 collective-permute-start.21
  608.9 67.3 %psum.175 = f32[]{:T(128)} all-reduce(f32[]{:T(128)} %get-tuple-element.42), channel_id=1, replica_groups=mesh['tx'=16,'ty'=8] {'tx','ty'}, use_global_device_ids=true, to_apply=%region_16.0 | all-reduce | flops 1 | bytes 8 | tf_op jit(solution)/shard_map/psum | solution.py:102
  678.2 62.9 %psum.176 = f32[]{:T(128)} all-reduce(f32[]{:T(128)} %get-tuple-element.40), channel_id=1, replica_groups=mesh['tx'=16,'ty'=8] {'tx','ty'}, use_global_device_ids=true, to_apply=%region_18.0 | all-reduce | flops 1 | bytes 8 | tf_op jit(solution)/shard_map/psum | solution.py:74
  757.0 67.7 %psum.177 = f32[]{:T(128)} all-reduce(f32[]{:T(128)} %get-tuple-element.38), channel_id=1, replica_groups=mesh['tx'=16,'ty'=8] {'tx','ty'}, use_global_device_ids=true, to_apply=%region_20.0 | all-reduce | flops 1 | bytes 8 | tf_op jit(solution)/shard_map/psum | solution.py:102
  826.6 62.6 %psum.178 = f32[]{:T(128)} all-reduce(f32[]{:T(128)} %get-tuple-element.36), channel_id=1, replica_groups=mesh['tx'=16,'ty'=8] {'tx','ty'}, use_global_device_ids=true, to_apply=%region_22.0 | all-reduce | flops 1 | bytes 8 | tf_op jit(solution)/shard_map/psum | solution.py:74
  905.4 67.1 %psum.179 = f32[]{:T(128)} all-reduce(f32[]{:T(128)} %get-tuple-element.34), channel_id=1, replica_groups=mesh['tx'=16,'ty'=8] {'tx','ty'}, use_global_device_ids=true, to_apply=%region_24.0 | all-reduce | flops 1 | bytes 8 | tf_op jit(solution)/shard_map/psum | solution.py:102
  974.5 63.6 %psum.180 = f32[]{:T(128)} all-reduce(f32[]{:T(128)} %get-tuple-element.32), channel_id=1, replica_groups=mesh['tx'=16,'ty'=8] {'tx','ty'}, use_global_device_ids=true, to_apply=%region_26.0 | all-reduce | flops 1 | bytes 8 | tf_op jit(solution)/shard_map/psum | solution.py:74
  1053.9 67.4 %psum.181 = f32[]{:T(128)} all-reduce(f32[]{:T(128)} %get-tuple-element.30), channel_id=1, replica_groups=mesh['tx'=16,'ty'=8] {'tx','ty'}, use_global_device_ids=true, to_apply=%region_28.0 | all-reduce | flops 1 | bytes 8 | tf_op jit(solution)/shard_map/psum | solution.py:102
  1123.3 63.0 %psum.182 = f32[]{:T(128)} all-reduce(f32[]{:T(128)} %get-tuple-element.28), channel_id=1, replica_groups=mesh['tx'=16,'ty'=8] {'tx','ty'}, use_global_device_ids=true, to_apply=%region_30.0 | all-reduce | flops 1 | bytes 8 | tf_op jit(solution)/shard_map/psum | solution.py:74
  1202.0 67.7 %psum.183 = f32[]{:T(128)} all-reduce(f32[]{:T(128)} %get-tuple-element.26), channel_id=1, replica_groups=mesh['tx'=16,'ty'=8] {'tx','ty'}, use_global_device_ids=true, to_apply=%region_32.0 | all-reduce | flops 1 | bytes 8 | tf_op jit(solution)/shard_map/psum | solution.py:102
  1271.8 62.7 %psum.184 = f32[]{:T(128)} all-reduce(f32[]{:T(128)} %get-tuple-element.24), channel_id=1, replica_groups=mesh['tx'=16,'ty'=8] {'tx','ty'}, use_global_device_ids=true, to_apply=%region_34.0 | all-reduce | flops 1 | bytes 8 | tf_op jit(solution)/shard_map/psum | solution.py:74
  1352.2 67.3 %psum.185 = f32[]{:T(128)} all-reduce(f32[]{:T(128)} %get-tuple-element.22), channel_id=1, replica_groups=mesh['tx'=16,'ty'=8] {'tx','ty'}, use_global_device_ids=true, to_apply=%region_36.0 | all-reduce | flops 1 | bytes 8 | tf_op jit(solution)/shard_map/psum | solution.py:102
  1423.0 62.8 %psum.186 = f32[]{:T(128)} all-reduce(f32[]{:T(128)} %get-tuple-element.20), channel_id=1, replica_groups=mesh['tx'=16,'ty'=8] {'tx','ty'}, use_global_device_ids=true, to_apply=%region_38.0 | all-reduce | flops 1 | bytes 8 | tf_op jit(solution)/shard_map/psum | solution.py:74
  1504.0 67.7 %psum.187 = f32[]{:T(128)} all-reduce(f32[]{:T(128)} %get-tuple-element.18), channel_id=1, replica_groups=mesh['tx'=16,'ty'=8] {'tx','ty'}, use_global_device_ids=true, to_apply=%region_40.0 | all-reduce | flops 1 | bytes 8 | tf_op jit(solution)/shard_map/psum | solution.py:102
  1575.2 62.6 %psum.188 = f32[]{:T(128)} all-reduce(f32[]{:T(128)} %get-tuple-element.16), channel_id=1, replica_groups=mesh['tx'=16,'ty'=8] {'tx','ty'}, use_global_device_ids=true, to_apply=%region_42.0 | all-reduce | flops 1 | bytes 8 | tf_op jit(solution)/shard_map/psum | solution.py:74
  1656.4 67.2 %psum.189 = f32[]{:T(128)} all-reduce(f32[]{:T(128)} %get-tuple-element.14), channel_id=1, replica_groups=mesh['tx'=16,'ty'=8] {'tx','ty'}, use_global_device_ids=true, to_apply=%region_44.0 | all-reduce | flops 1 | bytes 8 | tf_op jit(solution)/shard_map/psum | solution.py:102
  1726.4 63.6 %psum.190 = f32[]{:T(128)} all-reduce(f32[]{:T(128)} %multiply_reduce_fusion.1), channel_id=1, replica_groups=mesh['tx'=16,'ty'=8] {'tx','ty'}, use_global_device_ids=true, to_apply=%region_46.0 | all-reduce | flops 1 | bytes 8 | tf_op jit(solution)/shard_map/psum | solution.py:74
  1808.5 67.3 %psum.191 = f32[]{:T(128)} all-reduce(f32[]{:T(128)} %fusion.38), channel_id=1, replica_groups=mesh['tx'=16,'ty'=8] {'tx','ty'}, use_global_device_ids=true, to_apply=%region_48.0 | all-reduce | flops 1 | bytes 8 | tf_op jit(solution)/shard_map/psum | solution.py:102
  (243 shorter events, 253.1 us)
Async XLA Ops:
  20.2 25.6 %collective-permute-start = (bf16[151,1,128]{2,0,1:T(8,128)(2,1)S(1)}, bf16[151,1,128]{2,0,1:T(8,128)(2,1)S(1)}, u32[]{:S(2)}, u32[]{:S(2)}) collective-permute-start(bf16[151,1,128]{2,0,1:T(8,128)(2,1)S(1)} %copy.84), channel_id=1, source_target_pairs={{0,8},{8,16},{16,24},{24,32},{32,40},{40,48},{48,56},{56,64},{64,7... | collective-permute-start | bytes 115976 | tf_op jit(solution)/shard_map/ppermute | solution.py:16
  28.2 21.3 %collective-permute-start.1 = (bf16[151,1,128]{2,0,1:T(8,128)(2,1)S(1)}, bf16[151,1,128]{2,0,1:T(8,128)(2,1)S(1)}, u32[]{:S(2)}, u32[]{:S(2)}) collective-permute-start(bf16[151,1,128]{2,0,1:T(8,128)(2,1)S(1)} %copy.85), channel_id=1, source_target_pairs={{8,0},{16,8},{24,16},{32,24},{40,32},{48,40},{56,48},{64,56},{72,6... | collective-permute-start | bytes 115976 | tf_op jit(solution)/shard_map/ppermute | solution.py:17
  30.5 9.3 collective-permute-start.4
  31.8 11.0 collective-permute-start.5
  55.4 14.9 collective-permute-start.2
  60.4 10.0 collective-permute-start.3
  64.5 40.6 %collective-permute-start.6 = (f32[50,66,1]{1,2,0:T(1,128)}, f32[50,66,1]{1,2,0:T(1,128)}, u32[]{:S(2)}, u32[]{:S(2)}) collective-permute-start(f32[50,66,1]{1,2,0:T(1,128)} %get-tuple-element.65), channel_id=1, source_target_pairs={{1,0},{2,1},{3,2},{4,3},{5,4},{6,5},{7,6},{9,8},{10,9},{11,10},{12... | collective-permute-start | bytes 39608 | tf_op jit(solution)/shard_map/ppermute | solution.py:17
  66.4 38.7 %collective-permute-start.7 = (f32[50,66,1]{1,2,0:T(1,128)}, f32[50,66,1]{1,2,0:T(1,128)}, u32[]{:S(2)}, u32[]{:S(2)}) collective-permute-start(f32[50,66,1]{1,2,0:T(1,128)} %get-tuple-element.66), channel_id=1, source_target_pairs={{0,1},{1,2},{2,3},{3,4},{4,5},{5,6},{6,7},{8,9},{9,10},{10,11},{11... | collective-permute-start | bytes 39608 | tf_op jit(solution)/shard_map/ppermute | solution.py:16
  138.6 5.6 collective-permute-start.8
  139.9 5.8 collective-permute-start.9
  146.4 6.4 collective-permute-start.10
  297.4 5.3 collective-permute-start.13
  302.8 6.6 collective-permute-start.14
  447.2 5.3 collective-permute-start.17
  452.6 6.1 collective-permute-start.18
  595.5 5.3 collective-permute-start.21
  600.9 6.5 collective-permute-start.22
  743.8 5.3 collective-permute-start.25
  749.2 6.3 collective-permute-start.26
  892.0 5.3 collective-permute-start.29
  897.4 6.5 collective-permute-start.30
  1040.8 5.3 collective-permute-start.33
  1046.2 5.8 collective-permute-start.34
  1189.1 5.3 collective-permute-start.37
  1194.5 6.1 collective-permute-start.38
  1336.0 5.6 collective-permute-start.40
  1337.5 5.3 collective-permute-start.41
  1342.9 6.3 collective-permute-start.42
  1489.4 5.3 collective-permute-start.45
  1494.7 6.3 collective-permute-start.46
  1646.7 6.7 collective-permute-start.50
  1799.0 5.8 collective-permute-start.54
  (48 other events, 6167.9 us)
where the time goes:
time: 1900 us; the launch traced here: 1880 us
  blocking collectives  1510 us (79%)
  starting transfers between devices  162 us (9%)
  other arithmetic  112 us (6%)
  local copies, waits for them, and re-layouts  46 us (2%)
  between operations  32.8 us (2%)
  waiting for transfers between devices  24.5 us (1%)
    psum x12, blocking collectives, squares_total(): return lax.psum(jnp.sum(residual * residual), ('tx', 'ty'))  766 us
    psum x11, blocking collectives, on_device(): alpha = norm_now / lax.psum(jnp.sum(direction * image), ('tx', 'ty'))  742 us
    ppermute x28, starting transfers between devices, extended(): before = lax.ppermute(last, axis, up)  97.2 us
    ppermute x28, starting transfers between devices, extended(): after = lax.ppermute(initial, axis, down)  65.1 us
  transfers between devices with their start and end apart: 56, of which 24 were waited for; matrix products, arithmetic and copies ran while one was open for 3% of the time, Pallas kernels for 0%

commit v1 on v0

v1 whole, which is shorter than its diff:
```python
import jax
import jax.numpy as jnp
from jax import lax
from jax.experimental import pallas as pl
from jax.experimental.pallas import tpu as pltpu
from jax.sharding import PartitionSpec as P

ITERS = 12
LEVELS = 50
LP = 56
NX, NY = 64, 128
LB = 10
HALO = 12
LOW, HIGH = 0.7, 31.0
MID, HALF = 0.5 * (HIGH + LOW), 0.5 * (HIGH - LOW)
GUARD = 1.0e5
F32 = jnp.float32


def lanes(shape):
    return lax.broadcasted_iota(jnp.int32, shape, len(shape) - 1)


def rows_of(shape):
    return lax.broadcasted_iota(jnp.int32, shape, len(shape) - 2)


def roll(x, shift, axis):
    return pltpu.roll(x, shift % x.shape[axis], axis)


def half_kappa(theta, scale):
    return 0.025 * (1.5 + jnp.tanh(theta.astype(F32) * scale))


def interior_kernel(
    scale, weight, lam, lam_next, theta, theta_next, vel_u, vel_v, mask, column,
    stepped, sent, edge_rows, rhs, coupled, weights_out, flux,
):
    step = pl.program_id(0)
    tile = (NX, NY)
    lane, row = lanes(tile), rows_of(tile)
    wet = mask[...].astype(F32)

    @pl.when(step == 0)
    def _():
        sent[...] = jnp.zeros_like(sent)
        edge_rows[...] = jnp.zeros_like(edge_rows)
        rhs[...] = jnp.zeros_like(rhs)
        flux[...] = jnp.zeros_like(flux)
        weights_out[...] = jnp.zeros_like(weights_out)
        coupled[...] = wet * column[...]

    face_x = jnp.where(row == NX - 1, 0.0, wet * roll(wet, -1, 0))
    face_y = jnp.where(lane == NY - 1, 0.0, wet * roll(wet, -1, 1))
    half = half_kappa(theta[0], scale[0, step * LB])
    below = flux[...]
    total = rhs[...]
    for kk in range(LB):
        k = step * LB + kk
        w = weight[k]
        here = lam[kk]
        if kk + 1 < LB:
            above = lam[kk + 1]
            half_above = half_kappa(theta[kk + 1], scale[0, k + 1])
        else:
            above = lam_next[0]
            half_above = half_kappa(theta_next[0], scale[0, jnp.minimum(k + 1, LEVELS - 1)])
        half_u = vel_u[kk].astype(F32) * (0.5 * scale[1, k])
        half_v = vel_v[kk].astype(F32) * (0.5 * scale[2, k])
        dx = face_x * (roll(here, -1, 0) - here)
        sx = half + roll(half, -1, 0)
        dy = face_y * (roll(here, -1, 1) - here)
        sy = half + roll(half, -1, 1)
        vertical = (half + half_above) * (above - here)
        value = here + dx * (sx + half_u) + roll(dx * (half_u - sx), 1, 0)
        value = value + dy * (sy + half_v) + roll(dy * (half_v - sy), 1, 1)
        value = wet * (value + (vertical - below))
        stepped[kk] = value
        total = total + w * value
        at = 16 + 2 * k
        pair = (lane == at) | (lane == at + 1)
        shift = at + 1
        sent[0:64] = jnp.where(pair, pltpu.roll(here, shift, 1), sent[0:64])
        sent[64:128] = jnp.where(pair, pltpu.roll(half, shift, 1), sent[64:128])
        sent[128:192] = jnp.where(lane == at, pltpu.roll(half_v, shift, 1), sent[128:192])
        edge_rows[0, pl.ds(k, 1), :] = here[NX - 1 :]
        edge_rows[1, pl.ds(k, 1), :] = half[NX - 1 :]
        edge_rows[2, pl.ds(k, 1), :] = half_u[NX - 1 :]
        edge_rows[3, pl.ds(k, 1), :] = here[:1]
        edge_rows[4, pl.ds(k, 1), :] = half[:1]
        weights_out[pl.ds(k, 1), :] = jnp.full((1, NY), w, F32)
        lane8 = lanes((8, NY))
        weights_out[LP : LP + 8, :] = jnp.where(
            (lane8 == at) | (lane8 == at + 1), w, weights_out[LP : LP + 8, :]
        )
        below, half = vertical, half_above
    flux[...] = below
    rhs[...] = total

    @pl.when(step == LEVELS // LB - 1)
    def _():
        rim = (lane < HALO) | (lane >= NY - HALO)
        sent[0:64] = jnp.where(rim, total, sent[0:64])
        sent[64:128] = jnp.where(rim, coupled[...], sent[64:128])
        lane_e = lanes((LP, NY))
        packed = jnp.where((lane_e < HALO) | (lane_e >= NY - HALO), edge_rows[0], 0.0)
        for m in range(1, 5):
            inside = (lane_e >= 24 * m - HALO) & (lane_e < 24 * m + HALO)
            packed = jnp.where(inside, roll(edge_rows[m], 24 * m, 1), packed)
        sent[192 : 192 + LP] = packed


def column_kernel(
    from_south, from_north, sent, edge_rows, rhs, coupled, weights,
    down, up, rhs_out, outer, correction,
):
    j = lax.axis_index("ty")
    has_south = jnp.where(j > 0, 1.0, 0.0)
    has_north = jnp.where(j < lax.axis_size("ty") - 1, 1.0, 0.0)
    tile = (NX, NY)
    lane = lanes(tile)
    even = (lane & 1) == 0
    first, last = lane < HALO, lane >= NY - HALO
    south_c = from_south[64:128] * has_south
    north_c = from_north[64:128] * has_north
    outer_c = jnp.where(first, north_c, jnp.where(last, south_c, 0.0))
    outer_r = jnp.where(
        first, from_north[0:64] * has_north, jnp.where(last, from_south[0:64] * has_south, 0.0)
    )
    own_c = coupled[...]
    wet = jnp.where(own_c > 0.0, 1.0, 0.0)
    outer_wet = jnp.where(outer_c > 0.0, 1.0, 0.0)
    mask = jnp.where(
        even, wet[:, NY - 1 :] * outer_wet[:, :1], wet[:, :1] * outer_wet[:, NY - 1 :]
    )
    lam = jnp.where(even, roll(from_north[0:64], -1, 1), roll(from_south[0:64], 1, 1))
    half = jnp.where(even, roll(from_north[64:128], -1, 1), roll(from_south[64:128], 1, 1))
    speed = jnp.where(even, sent[128:192], -roll(from_south[128:192], 1, 1))
    gradient = mask * (lam - sent[0:64])
    both = half + sent[64:128]
    levels = (lane >= 16) & (lane < 16 + 2 * LEVELS)
    mine = jnp.where(levels, gradient * (both + speed), 0.0)
    theirs = jnp.where(levels, gradient * (speed - both), 0.0)
    correction[...] = mine
    w = weights[LP : LP + 1, :]

    def total(values, which):
        return jnp.sum(jnp.where(which, w * values, 0.0), axis=1, keepdims=True)

    odd = jnp.logical_not(even)
    own = rhs[...]
    own = own + jnp.where(lane == NY - 1, total(mine, even), 0.0)
    own = own + jnp.where(lane == 0, total(mine, odd), 0.0)
    outer_r = outer_r + jnp.where(lane == 0, total(theirs, even), 0.0)
    outer_r = outer_r + jnp.where(lane == NY - 1, total(theirs, odd), 0.0)
    rhs_out[...] = own
    outer[0:64] = outer_r
    outer[64:128] = outer_c
    lane_e = lanes((LP, NY))
    north = (lane_e >= 0) & (lane_e < HALO)
    for m in range(1, 5):
        north = north | ((lane_e >= 24 * m) & (lane_e < 24 * m + HALO))
    levels_outer = jnp.where(north, from_north[192 : 192 + LP], from_south[192 : 192 + LP])
    strip_lane = lanes((16, NY))
    window = (strip_lane >= HALO) & (strip_lane < 3 * HALO)

    def strips(out, at, start):
        out[at : at + LP] = levels_outer
        out[at + LP : at + LP + 16] = own[start : start + 16]
        out[at + LP + 16 : at + LP + 32] = own_c[start : start + 16]
        out[at + LP + 32 : at + LP + 48] = jnp.where(
            window, roll(outer_c[start : start + 16], 24, 1), outer_r[start : start + 16]
        )

    for m in range(3):
        down[m * LP : (m + 1) * LP] = edge_rows[m]
    strips(down, 3 * LP, NX - 16)
    for m in range(2):
        up[m * LP : (m + 1) * LP] = edge_rows[3 + m]
    strips(up, 2 * LP, 0)


def basis_kernel(
    from_up, from_down, down, up, rhs, coupled, outer, weights,
    basis, dots, correction, rhs_out, parts,
):
    i = lax.axis_index("tx")
    has_up = jnp.where(i > 0, 1.0, 0.0)
    has_down = jnp.where(i < lax.axis_size("tx") - 1, 1.0, 0.0)
    w = weights[0:LP]
    lane16 = lanes((16, NY))
    rim16 = (lane16 < HALO) | (lane16 >= NY - HALO)

    def unpack(ref, count, m):
        return roll(ref[count * LP : (count + 1) * LP], -24 * m, 1)

    def strip(ref, count, has):
        at = (count + 1) * LP
        packed = ref[at + 32 : at + 48]
        return (
            (ref[at : at + 16] * has, jnp.where(rim16, packed, 0.0) * has),
            (ref[at + 16 : at + 32] * has, jnp.where(rim16, roll(packed, -24, 1), 0.0) * has),
        )

    up_r, up_c = strip(from_up, 3, has_up)
    down_r, down_c = strip(from_down, 2, has_down)
    own_r = [rhs[...], outer[0:64]]
    own_c = [coupled[...], outer[64:128]]

    def wet_of(value):
        return jnp.where(value > 0.0, 1.0, 0.0)

    row64 = rows_of((NX, NY))
    row16 = rows_of((16, NY))
    columns_r, columns_c = [], []
    for g in range(2):
        if g == 0:
            lam_u, half_u, speed_u = (from_up[m * LP : (m + 1) * LP] for m in range(3))
            lam_l, half_l, speed_l = (down[m * LP : (m + 1) * LP] for m in range(3))
            lam_d, half_d = (from_down[m * LP : (m + 1) * LP] for m in range(2))
            lam_f, half_f = (up[m * LP : (m + 1) * LP] for m in range(2))
        else:
            lam_u, half_u, speed_u = (unpack(from_up, 3, m) for m in range(3))
            lam_l, half_l, speed_l = (unpack(down, 3, m) for m in range(3))
            lam_d, half_d = (unpack(from_down, 2, 3 + m) for m in range(2))
            lam_f, half_f = (unpack(down, 3, 3 + m) for m in range(2))
        mask = wet_of(own_c[g][0:1]) * wet_of(up_c[g][15:16])
        gradient = mask * (lam_u - lam_f)
        both = half_u + half_f
        mine_u = gradient * (both - speed_u)
        theirs_u = -gradient * (both + speed_u)
        mask = wet_of(own_c[g][NX - 1 :]) * wet_of(down_c[g][0:1])
        gradient = mask * (lam_d - lam_l)
        both = half_d + half_l
        mine_d = gradient * (both + speed_l)
        theirs_d = -gradient * (both - speed_l)
        if g == 0:
            correction[0:LP] = mine_u
            correction[LP : 2 * LP] = mine_d

        def total(values):
            return jnp.sum(w * values, axis=0, keepdims=True)

        own = own_r[g]
        own = own + jnp.where(row64 == 0, total(mine_u), 0.0)
        own = own + jnp.where(row64 == NX - 1, total(mine_d), 0.0)
        above = up_r[g] + jnp.where(row16 == 15, total(theirs_u), 0.0)
        below = down_r[g] + jnp.where(row16 == 0, total(theirs_d), 0.0)
        if g == 0:
            rhs_out[...] = own
        else:
            rim = (lanes((NX, NY)) < HALO) | (lanes((NX, NY)) >= NY - HALO)
            own = jnp.where(rim, own, 0.0)
            above = jnp.where(rim16, above, 0.0)
            below = jnp.where(rim16, below, 0.0)
        low = rows_of((8, NY)) < 4

        def extended(middle, before, after):
            mixed = jnp.where(low, after[8:16], before[0:8])
            return jnp.concatenate([middle, after[0:8], mixed, before[8:16]], axis=0)

        columns_r.append(extended(own, above, below))
        columns_c.append(extended(own_c[g], up_c[g], down_c[g]))
    v = jnp.concatenate(columns_r, axis=1)
    c = jnp.concatenate(columns_c, axis=1)
    wet = wet_of(c)
    face_x = wet * roll(wet, -1, 0)
    face_y = wet * roll(wet, -1, 1)
    degree = face_x + roll(face_x, 1, 0) + face_y + roll(face_y, 1, 1)
    diagonal = (c + 4.0 * degree - MID) * (2.0 / HALF)
    face_x = face_x * (-8.0 / HALF)
    face_y = face_y * (-8.0 / HALF)

    def apply(s):
        out = diagonal * s + face_x * roll(s, -1, 0) + roll(face_x * s, 1, 0)
        return out + face_y * roll(s, -1, 1) + roll(face_y * s, 1, 1)

    def dot(n, a, b):
        product = a[:NX, :NY] * b[:NX, :NY]
        part = product[0:8]
        for t in range(1, 8):
            part = part + product[8 * t : 8 * t + 8]
        parts[n : n + 1, :] = jnp.sum(part, axis=0, keepdims=True)

    parts[24:32, :] = jnp.zeros((8, NY), F32)
    before = v
    basis[0] = v[:NX, :NY]
    dot(0, v, v)
    now = 0.5 * apply(v)
    dot(1, before, now)
    for n in range(1, ITERS):
        basis[n] = now[:NX, :NY]
        dot(2 * n, now, now)
        after = apply(now) - before
        dot(2 * n + 1, now, after)
        before, now = now, after
    sums = jnp.sum(parts[...], axis=1, keepdims=True)
    shape = (32, NY)
    line = jnp.sum(jnp.where(lanes(shape) == rows_of(shape), sums, 0.0), axis=0, keepdims=True)
    dots[...] = jnp.broadcast_to(line, dots.shape)


def solve_kernel(
    weight, gathered, basis, stepped, edges_y, edges_x, mask,
    out, surface, flag, scaled,
):
    step = pl.program_id(0)

    @pl.when(step == 0)
    def _():
        line = jnp.sum(gathered[...], axis=0, keepdims=True)
        shape = (32, NY)
        column = jnp.sum(jnp.where(lanes(shape) == rows_of(shape), line, 0.0), axis=1, keepdims=True)
        d = jnp.broadcast_to(column, shape)[0:24]
        d0 = d[0:1]
        d = d / d0
        row = rows_of((24, NY))
        moment = jnp.where((row & 1) == 0, 2.0 * d - 1.0, 2.0 * d - d[1:2])
        moment = jnp.where(row < 2, d, moment)
        largest = jnp.maximum(jnp.max(jnp.abs(moment), axis=0, keepdims=True), 1.0)
        quarter = 0.5 * HALF
        row16 = rows_of((16, NY))
        r, p = moment, moment
        rc = jnp.where(row16 == 0, 1.0, 0.0)
        pc = rc
        xc = jnp.zeros((16, NY), F32)
        rr = jnp.ones((1, NY), F32)
        worst = jnp.ones((1, NY), F32)
        good = jnp.ones((1, NY), F32)
        for n in range(ITERS):
            shifted = jnp.where(row == 0, p[1:2], roll(p, 1, 0)) + roll(p, -1, 0)
            hp = MID * p + quarter * shifted
            alpha = r[n : n + 1] / hp[n : n + 1]
            good = jnp.where(alpha > 0.0, good, 0.0)
            xc = xc + alpha * pc
            if n == ITERS - 1:
                break
            fresh = r - alpha * hp
            lead = -alpha * (quarter * (2.0 if n == 0 else 1.0))
            beta = lead * fresh[n + 1 : n + 2] / r[n : n + 1]
            image = MID * pc + quarter * (
                roll(pc, 1, 0)
                + jnp.where(row16 == 1, pc[0:1], 0.0)
                + jnp.where(row16 == 15, 0.0, roll(pc, -1, 0))
            )
            rc = rc - alpha * image
            pc = rc + beta * pc
            p = fresh + beta * p
            r = fresh
            rr = rr * beta
            good = jnp.where(rr > 0.0, good, 0.0)
            size = jnp.sum(jnp.abs(rc), axis=0, keepdims=True)
            worst = jnp.maximum(worst, size * size / rr)
        good = jnp.where(worst * largest < GUARD, good, 0.0)
        x = jnp.zeros((NX, NY), F32)
        for n in range(ITERS):
            x = x + xc[n : n + 1] * basis[n]
        x = jnp.where(good > 0.0, x, 0.0)
        surface[...] = x
        scaled[...] = mask[...].astype(F32) * x
        flag[...] = jnp.broadcast_to(good, flag.shape).astype(jnp.int32)

    lane = lanes((NX, NY))
    wx = scaled[...]
    for kk in range(LB):
        k = step * LB + kk
        shifted = pltpu.roll(edges_y[...], 111 + 128 - 2 * k, 1)
        value = stepped[kk] - weight[k] * wx
        out[kk] = value + jnp.where((lane == 0) | (lane == NY - 1), shifted, 0.0)
        out[kk, 0:1, :] += edges_x[pl.ds(k, 1), :]
        out[kk, NX - 1 : NX, :] += edges_x[pl.ds(LP + k, 1), :]


def whole(shape):
    return pl.BlockSpec(shape, lambda *_: (0,) * len(shape))


def arrays(*shapes):
    return tuple(jax.ShapeDtypeStruct(s, F32) for s in shapes)


def extended(value, sides):
    for axis, dim in sides:
        size, length = (lax.axis_size(axis), value.shape[dim])
        up = [(i, i + 1) for i in range(size - 1)]
        down = [(j, i) for i, j in up]
        last = lax.slice_in_dim(value, length - 1, length, axis=dim)
        initial = lax.slice_in_dim(value, 0, 1, axis=dim)
        before = lax.ppermute(last, axis, up)
        after = lax.ppermute(initial, axis, down)
        value = jnp.concatenate([before, value, after], axis=dim)
    return value


def iterate(rhs, land_mask, column_weight):
    sides = (("tx", 0), ("ty", 1))
    wet = extended(land_mask.astype(F32), sides)
    mc = wet[1:-1, 1:-1]
    faces = [mc * wet[2:, 1:-1], mc * wet[:-2, 1:-1], mc * wet[1:-1, 2:], mc * wet[1:-1, :-2]]

    def image_of(s):
        p = extended(s, sides)
        total = faces[0] * (s - p[2:, 1:-1]) + faces[1] * (s - p[:-2, 1:-1])
        total = total + faces[2] * (s - p[1:-1, 2:]) + faces[3] * (s - p[1:-1, :-2])
        return column_weight * s + 4.0 * total

    def total_of(value):
        return lax.psum(jnp.sum(value), ("tx", "ty"))

    def body(_, carry):
        x, r, p, rr = carry
        image = image_of(p)
        alpha = rr / total_of(p * image)
        x, r = x + alpha * p, r - alpha * image
        fresh = total_of(r * r)
        return x, r, r + fresh / rr * p, fresh

    start = (jnp.zeros_like(rhs), rhs, rhs, total_of(rhs * rhs))
    return lax.fori_loop(0, ITERS, body, start)[0]


def on_device(
    adjoint_in, state_theta, state_u, state_v, level_scale, land_mask, level_weights, column_weight
):
    steps = LEVELS // LB
    smem = pl.BlockSpec(memory_space=pltpu.SMEM)
    block = pl.BlockSpec((LB, NX, NY), lambda i: (i, 0, 0))
    following = pl.BlockSpec(
        (1, NX, NY), lambda i: (jnp.minimum((i + 1) * LB, LEVELS - 1), 0, 0)
    )
    tile = (NX, NY)
    stepped, sent, edge_rows, rhs, coupled, weights = pl.pallas_call(
        interior_kernel,
        name="interior",
        grid=(steps,),
        in_specs=[smem, smem, block, following, block, following, block, block, whole(tile), whole(tile)],
        out_specs=(
            block, whole((192 + LP, NY)), whole((5, LP, NY)), whole(tile), whole(tile), whole((LP + 8, NY)),
        ),
        out_shape=arrays(
            (LEVELS, NX, NY), (192 + LP, NY), (5, LP, NY), tile, tile, (LP + 8, NY)
        ),
        scratch_shapes=[pltpu.VMEM(tile, F32)],
    )(
        level_scale, level_weights, adjoint_in, adjoint_in, state_theta, state_theta,
        state_u, state_v, land_mask, column_weight,
    )

    def ring(axis):
        n = lax.axis_size(axis)
        return [(i, (i + 1) % n) for i in range(n)], [((i + 1) % n, i) for i in range(n)]

    onward, back = ring("ty")
    from_south = lax.ppermute(sent, "ty", onward)
    from_north = lax.ppermute(sent, "ty", back)
    down, up, rhs, outer, edges_y = pl.pallas_call(
        column_kernel,
        name="columns",
        out_shape=arrays((4 * LP + 48, NY), (3 * LP + 48, NY), tile, (128, NY), tile),
    )(from_south, from_north, sent, edge_rows, rhs, coupled, weights)
    onward, back = ring("tx")
    from_up = lax.ppermute(down, "tx", onward)
    from_down = lax.ppermute(up, "tx", back)
    devices = lax.axis_size("tx") * lax.axis_size("ty")
    basis, dots, edges_x, rhs = pl.pallas_call(
        basis_kernel,
        name="basis",
        out_shape=arrays((ITERS, NX, NY), (devices, NY), (2 * LP, NY), tile),
        scratch_shapes=[pltpu.VMEM((32, NY), F32)],
    )(from_up, from_down, down, up, rhs, coupled, outer, weights)
    gathered = lax.all_to_all(dots, ("tx", "ty"), 0, 0, tiled=True)
    out, surface, flag = pl.pallas_call(
        solve_kernel,
        name="solve",
        grid=(steps,),
        in_specs=[
            smem, whole((devices, NY)), whole((ITERS, NX, NY)), block, whole(tile), whole((2 * LP, NY)), whole(tile),
        ],
        out_specs=(block, whole(tile), whole((8, NY))),
        out_shape=arrays((LEVELS, NX, NY), tile) + (jax.ShapeDtypeStruct((8, NY), jnp.int32),),
        scratch_shapes=[pltpu.VMEM(tile, F32)],
    )(level_weights, gathered, basis, stepped, edges_y, edges_x, land_mask)

    def unsolved(carry):
        return carry[0] == 0

    def slow(carry):
        _, base, _ = carry
        x = iterate(rhs, land_mask, column_weight)
        scaled = land_mask.astype(F32) * x
        return jnp.int32(1), base - level_weights[:, None, None] * scaled[None], x

    _, out, surface = lax.while_loop(unsolved, slow, (flag[0, 0], out, surface))
    return (out, surface)


def solution(mesh):
    field, plane = P(None, "tx", "ty"), P("tx", "ty")
    return jax.shard_map(
        on_device,
        mesh=mesh,
        in_specs=(field, field, field, field, P(), plane, P(), plane),
        out_specs=(field, plane),
        check_vma=False,
    )
```

time: 1900 us -> 58.6 us (0.03)
  blocking collectives: 1510 us -> 21.5 us
  starting transfers between devices: 162 us -> 8.07 us
  other arithmetic: 112 us -> 0 us
  local copies, waits for them, and re-layouts: 46 us -> 3.67 us
  between operations: 32.8 us -> 0.68 us
    psum x23 -> x0, blocking collectives: 1510 us -> none  [the longest x12 766 us: squares_total(): return lax.psum(jnp.sum(residual * residual), ('tx', 'ty'))]
    ppermute x56 -> x4, starting transfers between devices: 162 us -> 8.07 us  [the longest x1 3.8 us: on_device(): from_down = lax.ppermute(up, 'tx', back)]
    reduce_sum x24 -> x0, other arithmetic: 61.8 us -> none  [the longest x1 32.4 us: on_device(): rhs = jnp.sum(level_weights[:, None, None] * stepped, axis=0)]
    concatenate x2 -> x0, other arithmetic: 29.4 us -> none  [the longest x1 26.7 us: extended(): value = jnp.concatenate([before, value, after], axis=dim)]
    all_to_all x0 -> x1, blocking collectives: none -> 21.5 us  [on_device(): gathered = lax.all_to_all(dots, ('tx', 'ty'), 0, 0, tiled=True)]
    ppermute x56 -> x4, waiting for transfers between devices: 24.5 us -> 5.54 us  [the longest x1 2.79 us: on_device(): from_north = lax.ppermute(sent, 'ty', back)]
  transfers between devices with their start and end apart: 56 -> 4, of which waited for: 24 -> 4; matrix products, arithmetic and copies ran while one was open for 3% -> 0% of each run, Pallas kernels for 0% -> 0%
where the time goes in v1:
time: 58.6 us; the launch traced here: 58.2 us
  blocking collectives  21.5 us (37%)
  Pallas kernels  18.1 us (31%)
  starting transfers between devices  8.07 us (14%)
  waiting for transfers between devices  5.54 us (9%)
  local copies, waits for them, and re-layouts  3.67 us (6%)
  between operations  0.68 us (1%)
  loops' own time  0.65 us (1%)
    all_to_all x1, blocking collectives, on_device(): gathered = lax.all_to_all(dots, ('tx', 'ty'), 0, 0, tiled=True)  21.5 us
    pallas_call x1, Pallas kernels, on_device(): pl.pallas_call(interior_kernel, name='interior', grid=(steps,), in_specs=...  8.24 us
    pallas_call x1, Pallas kernels, on_device(): pl.pallas_call(solve_kernel, name='solve', grid=(steps,), in_specs=[smem,...  4.56 us
    ppermute x1, starting transfers between devices, on_device(): from_down = lax.ppermute(up, 'tx', back)  3.8 us
    pallas_call x1, Pallas kernels, on_device(): pl.pallas_call(basis_kernel, name='basis', out_shape=arrays((ITERS, NX, N...  3.14 us
    ppermute x1, waiting for transfers between devices, on_device(): from_north = lax.ppermute(sent, 'ty', back)  2.79 us
    unnamed x16, local copies, waits for them, and re-layouts  2.48 us
    pallas_call x1, Pallas kernels, on_device(): pl.pallas_call(column_kernel, name='columns', out_shape=arrays((4 * LP +...  2.13 us
  transfers between devices with their start and end apart: 4, of which 4 were waited for; matrix products, arithmetic and copies ran while one was open for 0% of the time, Pallas kernels for 0%

profile of v1, /device:TPU:1, one launch (start us, length us, event | category | flops | bytes accessed | tf_op | source)
XLA Modules:
  0.0 58.2 jit_solution(1429776998007359923)
XLA Ops:
  0.6 0.0 copy-start.8
  0.6 0.0 copy-start.3
  0.7 8.2 %interior.1 = (f32[50,64,128]{2,1,0:T(8,128)}, f32[248,128]{1,0:T(8,128)}, f32[5,56,128]{2,1,0:T(8,128)}, f32[64,128]{1,0:T(8,128)}, f32[64,128]{1,0:T(8,128)}, /*index=5*/f32[64,128]{1,0:T(8,128)}) custom-call(f32[3,50]{1,0:T(4,128)} %scale.1, f32[50]{0:T(128)} %weight.3, f32[50,64,128]{2,1,0:T(8,128)} %lam_next.1, f32[50,64,128]{2,1,0:T(8,128)} %lam_next.1, ...), custom_call_target="tpu_custom_call" | custom-call | tf_op jit(solution)/shard_map/interior/pallas_call | solution.py:433
  8.9 1.4 %collective-permute-start.9 = (f32[248,128]{1,0:T(8,128)}, f32[248,128]{1,0:T(8,128)S(1)}, u32[]{:S(2)}, u32[]{:S(2)}) collective-permute-start(f32[248,128]{1,0:T(8,128)} %get-tuple-element.133.sent), channel_id=1, source_target_pairs={{1,0},{2,1},{3,2},{4,3},{5,4},{6,5},{7,6},{0,7},{9,8},{10,9},{11,1... | collective-permute-start | bytes 380936 | tf_op jit(solution)/shard_map/ppermute | solution.py:456
  10.3 1.6 %collective-permute-start.8 = (f32[248,128]{1,0:T(8,128)}, f32[248,128]{1,0:T(8,128)S(1)}, u32[]{:S(2)}, u32[]{:S(2)}) collective-permute-start(f32[248,128]{1,0:T(8,128)} %get-tuple-element.133.sent), channel_id=1, source_target_pairs={{0,1},{1,2},{2,3},{3,4},{4,5},{5,6},{6,7},{7,0},{8,9},{9,10},{10,1... | collective-permute-start | bytes 380936 | tf_op jit(solution)/shard_map/ppermute | solution.py:455
  12.0 2.8 %collective-permute-done.9.from_north = f32[248,128]{1,0:T(8,128)S(1)} collective-permute-done((f32[248,128]{1,0:T(8,128)}, f32[248,128]{1,0:T(8,128)S(1)}, u32[]{:S(2)}, u32[]{:S(2)}) %collective-permute-start.9) | collective-permute-done | bytes 127008 | tf_op jit(solution)/shard_map/ppermute | solution.py:456
  14.8 0.0 copy-start.5
  14.8 0.2 collective-permute-done.8.from_south
  14.9 0.0 copy-start.6
  14.9 0.5 copy-done.5
  15.4 0.2 copy-done.6
  15.6 2.1 %columns.1 = (f32[272,128]{1,0:T(8,128)}, f32[216,128]{1,0:T(8,128)}, f32[64,128]{1,0:T(8,128)}, f32[128,128]{1,0:T(8,128)}, f32[64,128]{1,0:T(8,128)}) custom-call(f32[248,128]{1,0:T(8,128)} %copy-done.6, f32[248,128]{1,0:T(8,128)} %copy-done.5, f32[248,128]{1,0:T(8,128)} %get-tuple-element.133.sent, f32[5,56,128]{2,1,0:T(8,128)} %get-tuple-element.134.edge_rows, ...), custom_call_target="tpu_custom_call" | custom-call | tf_op jit(solution)/shard_map/columns/pallas_call | solution.py:457
  17.7 0.0 copy-start.2
  17.7 1.2 %collective-permute-start.10 = (f32[272,128]{1,0:T(8,128)}, f32[272,128]{1,0:T(8,128)S(1)}, u32[]{:S(2)}, u32[]{:S(2)}) collective-permute-start(f32[272,128]{1,0:T(8,128)} %get-tuple-element.138.down), channel_id=1, source_target_pairs={{0,8},{8,16},{16,24},{24,32},{32,40},{40,48},{48,56},{56,64},{64,7... | collective-permute-start | bytes 417800 | tf_op jit(solution)/shard_map/ppermute | solution.py:463
  18.9 3.8 %collective-permute-start.11 = (f32[216,128]{1,0:T(8,128)}, f32[216,128]{1,0:T(8,128)S(1)}, u32[]{:S(2)}, u32[]{:S(2)}) collective-permute-start(f32[216,128]{1,0:T(8,128)} %get-tuple-element.139.up), channel_id=1, source_target_pairs={{8,0},{16,8},{24,16},{32,24},{40,32},{48,40},{56,48},{64,56},{72,6... | collective-permute-start | bytes 331784 | tf_op jit(solution)/shard_map/ppermute | solution.py:464
  22.7 2.1 %collective-permute-done.11.from_down = f32[216,128]{1,0:T(8,128)S(1)} collective-permute-done((f32[216,128]{1,0:T(8,128)}, f32[216,128]{1,0:T(8,128)S(1)}, u32[]{:S(2)}, u32[]{:S(2)}) %collective-permute-start.11) | collective-permute-done | bytes 110624 | tf_op jit(solution)/shard_map/ppermute | solution.py:464
  24.8 0.0 copy-start.7
  24.8 0.5 collective-permute-done.10.from_up
  25.3 0.0 copy-start.4
  25.3 0.1 copy-done.7
  25.4 0.5 copy-done.4
  26.0 3.1 %basis.1 = (f32[12,64,128]{2,1,0:T(8,128)}, f32[128,128]{1,0:T(8,128)}, f32[112,128]{1,0:T(8,128)}, f32[64,128]{1,0:T(8,128)S(1)}) custom-call(f32[272,128]{1,0:T(8,128)} %copy-done.4, f32[216,128]{1,0:T(8,128)} %copy-done.7, f32[272,128]{1,0:T(8,128)} %get-tuple-element.138.down, f32[216,128]{1,0:T(8,128)} %get-tuple-element.139.up, ...), custom_call_target="tpu_custom_call" | custom-call | tf_op jit(solution)/shard_map/basis/pallas_call | solution.py:466
  29.1 21.5 %all_to_all.11 = f32[128,1,128]{2,1,0:T(1,128)} all-to-all(f32[128,1,128]{2,1,0:T(1,128)} %bitcast.6), channel_id=1, replica_groups=mesh['tx'=16,'ty'=8] {'tx','ty'}, dimensions={0} | all-to-all | bytes 131072 | tf_op jit(solution)/shard_map/all_to_all | solution.py:472
  50.6 0.0 copy-done.8
  50.6 0.0 copy-done.3
  50.6 4.6 %solve.1 = (f32[50,64,128]{2,1,0:T(8,128)S(1)}, f32[64,128]{1,0:T(8,128)}, s32[8,128]{1,0:T(8,128)}) custom-call(f32[50]{0:T(128)S(1)} %copy-done.8, f32[128,128]{1,0:T(8,128)} %bitcast.5, f32[12,64,128]{2,1,0:T(8,128)} %get-tuple-element.143.basis, f32[50,64,128]{2,1,0:T(8,128)} %get-tuple-element.144.stepped, f32[64,128]{1,0:T(8,128)} %get-tuple-element.145.edges_y, ...), custom_call_target="tpu_custom_call" | custom-call | tf_op jit(solution)/shard_map/solve/pallas_call | solution.py:473
  55.2 1.2 %slice.67 = s32[1,1]{1,0:T(1,128)} slice(s32[8,128]{1,0:T(8,128)} %get-tuple-element.147), slice={[0:1], [0:1]} | slice | bytes 8 | tf_op jit(solution)/shard_map/slice | solution.py:494
  56.4 0.0 copy-done.2
  56.4 0.7 %while.28 = (s32[]{:T(128)}, f32[50,64,128]{2,1,0:T(8,128)S(1)}, f32[64,128]{1,0:T(8,128)}, f32[50]{0:T(128)S(1)}, s32[64,128]{1,0:T(8,128)S(1)}, /*index=5*/f32...) while((s32[]{:T(128)}, f32[50,64,128]{2,1,0:T(8,128)S(1)}, f32[64,128]{1,0:T(8,128)}, f32[50]{0:T(128)S(1)}, ...), condition=%region_9.0_spmd, body=%region_0.0_spmd | while | flops 1262598 | bytes 4581516 | solution.py:494
  57.1 0.0 copy-start
  57.1 1.2 %copy-done = f32[50,64,128]{2,1,0:T(8,128)} copy-done((f32[50,64,128]{2,1,0:T(8,128)}, f32[50,64,128]{2,1,0:T(8,128)S(1)}, u32[]{:S(2)}) %copy-start) | copy-done | bytes 1638424
Async XLA Ops:
  0.6 50.0 %copy-start.8 = (f32[50]{0:T(128)S(1)}, f32[50]{0:T(128)}, u32[]{:S(2)}) copy-start(f32[50]{0:T(128)} %weight.3) | copy-start | bytes 604
  0.6 50.0 %copy-start.3 = (s32[64,128]{1,0:T(8,128)S(1)}, s32[64,128]{1,0:T(8,128)}, u32[]{:S(2)}) copy-start(s32[64,128]{1,0:T(8,128)} %mask.3) | copy-start | bytes 98308
  8.9 5.9 %collective-permute-start.9 = (f32[248,128]{1,0:T(8,128)}, f32[248,128]{1,0:T(8,128)S(1)}, u32[]{:S(2)}, u32[]{:S(2)}) collective-permute-start(f32[248,128]{1,0:T(8,128)} %get-tuple-element.133.sent), channel_id=1, source_target_pairs={{1,0},{2,1},{3,2},{4,3},{5,4},{6,5},{7,6},{0,7},{9,8},{10,9},{11,1... | collective-permute-start | bytes 380936 | tf_op jit(solution)/shard_map/ppermute | solution.py:456
  10.3 4.6 %collective-permute-start.8 = (f32[248,128]{1,0:T(8,128)}, f32[248,128]{1,0:T(8,128)S(1)}, u32[]{:S(2)}, u32[]{:S(2)}) collective-permute-start(f32[248,128]{1,0:T(8,128)} %get-tuple-element.133.sent), channel_id=1, source_target_pairs={{0,1},{1,2},{2,3},{3,4},{4,5},{5,6},{6,7},{7,0},{8,9},{9,10},{10,1... | collective-permute-start | bytes 380936 | tf_op jit(solution)/shard_map/ppermute | solution.py:455
  14.8 0.7 %copy-start.5 = (f32[248,128]{1,0:T(8,128)}, f32[248,128]{1,0:T(8,128)S(1)}, u32[]{:S(2)}) copy-start(f32[248,128]{1,0:T(8,128)S(1)} %collective-permute-done.9.from_north) | copy-start | bytes 380932
  14.9 0.6 %copy-start.6 = (f32[248,128]{1,0:T(8,128)}, f32[248,128]{1,0:T(8,128)S(1)}, u32[]{:S(2)}) copy-start(f32[248,128]{1,0:T(8,128)S(1)} %collective-permute-done.8.from_south) | copy-start | bytes 380932
  17.7 38.7 %copy-start.2 = (f32[64,128]{1,0:T(8,128)S(1)}, f32[64,128]{1,0:T(8,128)}, u32[]{:S(2)}) copy-start(f32[64,128]{1,0:T(8,128)} %column.1) | copy-start | bytes 98308
  17.7 7.6 %collective-permute-start.10 = (f32[272,128]{1,0:T(8,128)}, f32[272,128]{1,0:T(8,128)S(1)}, u32[]{:S(2)}, u32[]{:S(2)}) collective-permute-start(f32[272,128]{1,0:T(8,128)} %get-tuple-element.138.down), channel_id=1, source_target_pairs={{0,8},{8,16},{16,24},{24,32},{32,40},{40,48},{48,56},{56,64},{64,7... | collective-permute-start | bytes 417800 | tf_op jit(solution)/shard_map/ppermute | solution.py:463
  18.9 5.9 %collective-permute-start.11 = (f32[216,128]{1,0:T(8,128)}, f32[216,128]{1,0:T(8,128)S(1)}, u32[]{:S(2)}, u32[]{:S(2)}) collective-permute-start(f32[216,128]{1,0:T(8,128)} %get-tuple-element.139.up), channel_id=1, source_target_pairs={{8,0},{16,8},{24,16},{32,24},{40,32},{48,40},{56,48},{64,56},{72,6... | collective-permute-start | bytes 331784 | tf_op jit(solution)/shard_map/ppermute | solution.py:464
  24.8 0.6 %copy-start.7 = (f32[216,128]{1,0:T(8,128)}, f32[216,128]{1,0:T(8,128)S(1)}, u32[]{:S(2)}) copy-start(f32[216,128]{1,0:T(8,128)S(1)} %collective-permute-done.11.from_down) | copy-start | bytes 331780
  25.3 0.7 %copy-start.4 = (f32[272,128]{1,0:T(8,128)}, f32[272,128]{1,0:T(8,128)S(1)}, u32[]{:S(2)}) copy-start(f32[272,128]{1,0:T(8,128)S(1)} %collective-permute-done.10.from_up) | copy-start | bytes 417796
  57.1 1.2 %copy-start = (f32[50,64,128]{2,1,0:T(8,128)}, f32[50,64,128]{2,1,0:T(8,128)S(1)}, u32[]{:S(2)}) copy-start(f32[50,64,128]{2,1,0:T(8,128)S(1)} %get-tuple-element.388) | copy-start | bytes 4915204

commit v2 on v1

--- a/solution.py
+++ b/solution.py
@@ -359,7 +359,7 @@
         x = jnp.where(good > 0.0, x, 0.0)
         surface[...] = x
         scaled[...] = mask[...].astype(F32) * x
-        flag[...] = jnp.broadcast_to(good, flag.shape).astype(jnp.int32)
+        flag[0] = jnp.min(good).astype(jnp.int32)
 
     lane = lanes((NX, NY))
     wx = scaled[...]
@@ -378,6 +378,14 @@
 
 def arrays(*shapes):
     return tuple(jax.ShapeDtypeStruct(s, F32) for s in shapes)
+
+
+def on_chip(count):
+    return [pl.BlockSpec(memory_space=pltpu.VMEM)] * count
+
+
+def limit(mebibytes):
+    return pltpu.CompilerParams(vmem_limit_bytes=mebibytes << 20)
 
 
 def extended(value, sides):
@@ -430,18 +438,21 @@
         (1, NX, NY), lambda i: (jnp.minimum((i + 1) * LB, LEVELS - 1), 0, 0)
     )
     tile = (NX, NY)
+    adjoint_in, state_theta, state_u, state_v = (
+        pltpu.with_memory_space_constraint(x, pltpu.HBM)
+        for x in (adjoint_in, state_theta, state_u, state_v)
+    )
     stepped, sent, edge_rows, rhs, coupled, weights = pl.pallas_call(
         interior_kernel,
         name="interior",
         grid=(steps,),
-        in_specs=[smem, smem, block, following, block, following, block, block, whole(tile), whole(tile)],
-        out_specs=(
-            block, whole((192 + LP, NY)), whole((5, LP, NY)), whole(tile), whole(tile), whole((LP + 8, NY)),
-        ),
+        in_specs=[smem, smem, block, following, block, following, block, block] + on_chip(2),
+        out_specs=[block] + on_chip(5),
         out_shape=arrays(
             (LEVELS, NX, NY), (192 + LP, NY), (5, LP, NY), tile, tile, (LP + 8, NY)
         ),
         scratch_shapes=[pltpu.VMEM(tile, F32)],
+        compiler_params=limit(16),
     )(
         level_scale, level_weights, adjoint_in, adjoint_in, state_theta, state_theta,
         state_u, state_v, land_mask, column_weight,
@@ -457,6 +468,9 @@
     down, up, rhs, outer, edges_y = pl.pallas_call(
         column_kernel,
         name="columns",
+        in_specs=on_chip(7),
+        out_specs=on_chip(5),
+        compiler_params=limit(8),
         out_shape=arrays((4 * LP + 48, NY), (3 * LP + 48, NY), tile, (128, NY), tile),
     )(from_south, from_north, sent, edge_rows, rhs, coupled, weights)
     onward, back = ring("tx")
@@ -466,6 +480,9 @@
     basis, dots, edges_x, rhs = pl.pallas_call(
         basis_kernel,
         name="basis",
+        in_specs=on_chip(8),
+        out_specs=on_chip(4),
+        compiler_params=limit(8),
         out_shape=arrays((ITERS, NX, NY), (devices, NY), (2 * LP, NY), tile),
         scratch_shapes=[pltpu.VMEM((32, NY), F32)],
     )(from_up, from_down, down, up, rhs, coupled, outer, weights)
@@ -474,12 +491,15 @@
         solve_kernel,
         name="solve",
         grid=(steps,),
-        in_specs=[
-            smem, whole((devices, NY)), whole((ITERS, NX, NY)), block, whole(tile), whole((2 * LP, NY)), whole(tile),
-        ],
-        out_specs=(block, whole(tile), whole((8, NY))),
-        out_shape=arrays((LEVELS, NX, NY), tile) + (jax.ShapeDtypeStruct((8, NY), jnp.int32),),
+        in_specs=[smem] + on_chip(2) + [block] + on_chip(3),
+        out_specs=[block] + on_chip(1) + [smem],
+        out_shape=(
+            pltpu.HBM((LEVELS, NX, NY), F32),
+            jax.ShapeDtypeStruct(tile, F32),
+            jax.ShapeDtypeStruct((1,), jnp.int32),
+        ),
         scratch_shapes=[pltpu.VMEM(tile, F32)],
+        compiler_params=limit(8),
     )(level_weights, gathered, basis, stepped, edges_y, edges_x, land_mask)
 
     def unsolved(carry):
@@ -491,7 +511,7 @@
         scaled = land_mask.astype(F32) * x
         return jnp.int32(1), base - level_weights[:, None, None] * scaled[None], x
 
-    _, out, surface = lax.while_loop(unsolved, slow, (flag[0, 0], out, surface))
+    _, out, surface = lax.while_loop(unsolved, slow, (flag[0], out, surface))
     return (out, surface)
 
 

time: 58.6 us -> 49 us (0.84)
  Pallas kernels: 18.1 us -> 12.7 us
  local copies, waits for them, and re-layouts: 3.67 us -> 0.69 us
  blocking collectives: 21.5 us -> 20.9 us
    pallas_call x3, Pallas kernels: 9.83 us -> 5.41 us  [the longest x1 3.74 us: on_device(): pl.pallas_call(solve_kernel, name='solve', grid=(steps,), in_specs=[smem]...]
    unnamed x16 -> x8, local copies, waits for them, and re-layouts: 2.48 us -> 0.69 us
    slice x1 -> x0, local copies, waits for them, and re-layouts: 1.19 us -> none  [on_device(): _, out, surface = lax.while_loop(unsolved, slow, (flag[0, 0], out, surface))]
    pallas_call x1, Pallas kernels: 8.24 us -> 7.29 us  [on_device(): pl.pallas_call(interior_kernel, name='interior', grid=(steps,), in_specs=...]
    all_to_all x1, blocking collectives: 21.5 us -> 20.9 us  [on_device(): gathered = lax.all_to_all(dots, ('tx', 'ty'), 0, 0, tiled=True)]
where the time goes in v2:
time: 49 us; the launch traced here: 48.8 us
  blocking collectives  20.9 us (43%)
  Pallas kernels  12.7 us (26%)
  starting transfers between devices  8.15 us (17%)
  waiting for transfers between devices  5.13 us (10%)
  local copies, waits for them, and re-layouts  0.69 us (1%)
  between operations  0.67 us (1%)
  loops' own time  0.55 us (1%)
    all_to_all x1, blocking collectives, on_device(): gathered = lax.all_to_all(dots, ('tx', 'ty'), 0, 0, tiled=True)  20.9 us
    pallas_call x1, Pallas kernels, on_device(): pl.pallas_call(interior_kernel, name='interior', grid=(steps,), in_specs=...  7.29 us
    ppermute x1, starting transfers between devices, on_device(): from_down = lax.ppermute(up, 'tx', back)  3.8 us
    pallas_call x1, Pallas kernels, on_device(): pl.pallas_call(solve_kernel, name='solve', grid=(steps,), in_specs=[smem]...  3.74 us
    ppermute x1, waiting for transfers between devices, on_device(): from_north = lax.ppermute(sent, 'ty', back)  2.58 us
    ppermute x1, waiting for transfers between devices, on_device(): from_down = lax.ppermute(up, 'tx', back)  1.76 us
    ppermute x1, starting transfers between devices, on_device(): from_south = lax.ppermute(sent, 'ty', onward)  1.63 us
    ppermute x1, starting transfers between devices, on_device(): from_north = lax.ppermute(sent, 'ty', back)  1.43 us
  transfers between devices with their start and end apart: 4, of which 4 were waited for; matrix products, arithmetic and copies ran while one was open for 0% of the time, Pallas kernels for 0%

profile of v2, /device:TPU:1, one launch (start us, length us, event | category | flops | bytes accessed | tf_op | source)
XLA Modules:
  0.0 48.8 jit_solution(16587459475452023863)
XLA Ops:
  0.6 0.0 copy-start
  0.6 0.7 %copy-done = f32[3,50]{1,0:T(4,128)S(1)} copy-done((f32[3,50]{1,0:T(4,128)S(1)}, f32[3,50]{1,0:T(4,128)}, u32[]{:S(2)}) %copy-start) | copy-done | bytes 624
  1.3 0.0 copy-start.5
  1.3 0.0 copy-start.6
  1.3 7.3 %interior.1 = (f32[50,64,128]{2,1,0:T(8,128)S(1)}, f32[248,128]{1,0:T(8,128)S(1)}, f32[5,56,128]{2,1,0:T(8,128)S(1)}, f32[64,128]{1,0:T(8,128)S(1)}, f32[64,128]{1,0:T(8,128)S(1)}, /*index=5*/f32[64,128]{1,0:T(8,128)S(1)}) custom-call(f32[3,50]{1,0:T(4,128)S(1)} %copy-done, f32[50]{0:T(128)} %weight.3, f32[50,64,128]{2,1,0:T(8,128)} %lam_next.1, ...), custom_call_target="tpu_custom_call" | custom-call | tf_op jit(solution)/shard_map/interior/pallas_call | solution.py:445
  8.6 1.4 %collective-permute-start.9 = (f32[248,128]{1,0:T(8,128)S(1)}, f32[248,128]{1,0:T(8,128)S(1)}, u32[]{:S(2)}, u32[]{:S(2)}) collective-permute-start(f32[248,128]{1,0:T(8,128)S(1)} %get-tuple-element.133.sent), channel_id=1, source_target_pairs={{1,0},{2,1},{3,2},{4,3},{5,4},{6,5},{7,6},{0,7},{9,8},{10,9},{11,1... | collective-permute-start | bytes 380936 | tf_op jit(solution)/shard_map/ppermute | solution.py:467
  10.1 1.6 %collective-permute-start.8 = (f32[248,128]{1,0:T(8,128)S(1)}, f32[248,128]{1,0:T(8,128)S(1)}, u32[]{:S(2)}, u32[]{:S(2)}) collective-permute-start(f32[248,128]{1,0:T(8,128)S(1)} %get-tuple-element.133.sent), channel_id=1, source_target_pairs={{0,1},{1,2},{2,3},{3,4},{4,5},{5,6},{6,7},{7,0},{8,9},{9,10},{10,1... | collective-permute-start | bytes 380936 | tf_op jit(solution)/shard_map/ppermute | solution.py:466
  11.7 2.6 %collective-permute-done.9.from_north = f32[248,128]{1,0:T(8,128)S(1)} collective-permute-done((f32[248,128]{1,0:T(8,128)S(1)}, f32[248,128]{1,0:T(8,128)S(1)}, u32[]{:S(2)}, u32[]{:S(2)}) %collective-permute-start.9) | collective-permute-done | bytes 127008 | tf_op jit(solution)/shard_map/ppermute | solution.py:467
  14.3 0.2 collective-permute-done.8.from_south
  14.4 0.3 columns.1
  14.7 0.0 copy-start.4
  14.7 1.3 %collective-permute-start.10 = (f32[272,128]{1,0:T(8,128)S(1)}, f32[272,128]{1,0:T(8,128)S(1)}, u32[]{:S(2)}, u32[]{:S(2)}) collective-permute-start(f32[272,128]{1,0:T(8,128)S(1)} %get-tuple-element.138.down), channel_id=1, source_target_pairs={{0,8},{8,16},{16,24},{24,32},{32,40},{40,48},{48,56},{56,64},{64,7... | collective-permute-start | bytes 417800 | tf_op jit(solution)/shard_map/ppermute | solution.py:477
  16.0 3.8 %collective-permute-start.11 = (f32[216,128]{1,0:T(8,128)S(1)}, f32[216,128]{1,0:T(8,128)S(1)}, u32[]{:S(2)}, u32[]{:S(2)}) collective-permute-start(f32[216,128]{1,0:T(8,128)S(1)} %get-tuple-element.139.up), channel_id=1, source_target_pairs={{8,0},{16,8},{24,16},{32,24},{40,32},{48,40},{56,48},{64,56},{72,6... | collective-permute-start | bytes 331784 | tf_op jit(solution)/shard_map/ppermute | solution.py:478
  19.8 1.8 %collective-permute-done.11.from_down = f32[216,128]{1,0:T(8,128)S(1)} collective-permute-done((f32[216,128]{1,0:T(8,128)S(1)}, f32[216,128]{1,0:T(8,128)S(1)}, u32[]{:S(2)}, u32[]{:S(2)}) %collective-permute-start.11) | collective-permute-done | bytes 110624 | tf_op jit(solution)/shard_map/ppermute | solution.py:478
  21.6 0.6 %collective-permute-done.10.from_up = f32[272,128]{1,0:T(8,128)S(1)} collective-permute-done((f32[272,128]{1,0:T(8,128)S(1)}, f32[272,128]{1,0:T(8,128)S(1)}, u32[]{:S(2)}, u32[]{:S(2)}) %collective-permute-start.10) | collective-permute-done | bytes 139296 | tf_op jit(solution)/shard_map/ppermute | solution.py:477
  22.2 1.4 %basis.1 = (f32[12,64,128]{2,1,0:T(8,128)S(1)}, f32[128,128]{1,0:T(8,128)S(1)}, f32[112,128]{1,0:T(8,128)S(1)}, f32[64,128]{1,0:T(8,128)S(1)}) custom-call(f32[272,128]{1,0:T(8,128)S(1)} %collective-permute-done.10.from_up, f32[216,128]{1,0:T(8,128)S(1)} %collective-permute-done.11.from_down, f32[272,128]{1,0:T(8,128)S(1)} %get-tuple-element.138.down, ...), custom_call_target="tpu_custom_call" | custom-call | tf_op jit(solution)/shard_map/basis/pallas_call | solution.py:480
  23.6 20.9 %all_to_all.11 = f32[128,1,128]{2,1,0:T(1,128)S(1)} all-to-all(f32[128,1,128]{2,1,0:T(1,128)S(1)} %bitcast.6), channel_id=1, replica_groups=mesh['tx'=16,'ty'=8] {'tx','ty'}, dimensions={0} | all-to-all | bytes 131072 | tf_op jit(solution)/shard_map/all_to_all | solution.py:489
  44.5 0.0 copy-done.5
  44.5 0.0 copy-done.6
  44.5 3.7 %solve.1 = (f32[50,64,128]{2,1,0:T(8,128)}, f32[64,128]{1,0:T(8,128)}, s32[1]{0:T(128)}) custom-call(f32[50]{0:T(128)S(1)} %copy-done.6, f32[128,128]{1,0:T(8,128)S(1)} %bitcast.5, f32[12,64,128]{2,1,0:T(8,128)S(1)} %get-tuple-element.143.basis, f32[50,64,128]{2,1,0:T(8,128)S(1)} %get-tuple-element.144.stepped, f32[64,128]{1,0:T(8,128)S(1)} %get-tuple-element.145.edges_y, ...), custom_call_target="tpu_custom_call" | custom-call | tf_op jit(solution)/shard_map/solve/pallas_call | solution.py:490
  48.2 0.0 copy-done.4
  48.2 0.6 %while.28 = (s32[]{:T(128)}, f32[50,64,128]{2,1,0:T(8,128)}, f32[64,128]{1,0:T(8,128)}, f32[50]{0:T(128)S(1)}, s32[64,128]{1,0:T(8,128)S(1)}, /*index=5*/f32[64,...) while((s32[]{:T(128)}, f32[50,64,128]{2,1,0:T(8,128)}, f32[64,128]{1,0:T(8,128)}, f32[50]{0:T(128)S(1)}, ...), condition=%region_9.0_spmd, body=%region_0.0_spmd | while | flops 1262598 | bytes 17688772 | solution.py:514
Async XLA Ops:
  0.6 0.7 %copy-start = (f32[3,50]{1,0:T(4,128)S(1)}, f32[3,50]{1,0:T(4,128)}, u32[]{:S(2)}) copy-start(f32[3,50]{1,0:T(4,128)} %scale.1) | copy-start | bytes 1804
  1.3 43.1 %copy-start.5 = (s32[64,128]{1,0:T(8,128)S(1)}, s32[64,128]{1,0:T(8,128)}, u32[]{:S(2)}) copy-start(s32[64,128]{1,0:T(8,128)} %mask.3) | copy-start | bytes 98308
  1.3 43.1 %copy-start.6 = (f32[50]{0:T(128)S(1)}, f32[50]{0:T(128)}, u32[]{:S(2)}) copy-start(f32[50]{0:T(128)} %weight.3) | copy-start | bytes 604
  8.6 5.6 %collective-permute-start.9 = (f32[248,128]{1,0:T(8,128)S(1)}, f32[248,128]{1,0:T(8,128)S(1)}, u32[]{:S(2)}, u32[]{:S(2)}) collective-permute-start(f32[248,128]{1,0:T(8,128)S(1)} %get-tuple-element.133.sent), channel_id=1, source_target_pairs={{1,0},{2,1},{3,2},{4,3},{5,4},{6,5},{7,6},{0,7},{9,8},{10,9},{11,1... | collective-permute-start | bytes 380936 | tf_op jit(solution)/shard_map/ppermute | solution.py:467
  10.1 4.4 %collective-permute-start.8 = (f32[248,128]{1,0:T(8,128)S(1)}, f32[248,128]{1,0:T(8,128)S(1)}, u32[]{:S(2)}, u32[]{:S(2)}) collective-permute-start(f32[248,128]{1,0:T(8,128)S(1)} %get-tuple-element.133.sent), channel_id=1, source_target_pairs={{0,1},{1,2},{2,3},{3,4},{4,5},{5,6},{6,7},{7,0},{8,9},{9,10},{10,1... | collective-permute-start | bytes 380936 | tf_op jit(solution)/shard_map/ppermute | solution.py:466
  14.7 33.5 %copy-start.4 = (f32[64,128]{1,0:T(8,128)S(1)}, f32[64,128]{1,0:T(8,128)}, u32[]{:S(2)}) copy-start(f32[64,128]{1,0:T(8,128)} %column.1) | copy-start | bytes 98308
  14.7 7.4 %collective-permute-start.10 = (f32[272,128]{1,0:T(8,128)S(1)}, f32[272,128]{1,0:T(8,128)S(1)}, u32[]{:S(2)}, u32[]{:S(2)}) collective-permute-start(f32[272,128]{1,0:T(8,128)S(1)} %get-tuple-element.138.down), channel_id=1, source_target_pairs={{0,8},{8,16},{16,24},{24,32},{32,40},{40,48},{48,56},{56,64},{64,7... | collective-permute-start | bytes 417800 | tf_op jit(solution)/shard_map/ppermute | solution.py:477
  16.0 5.6 %collective-permute-start.11 = (f32[216,128]{1,0:T(8,128)S(1)}, f32[216,128]{1,0:T(8,128)S(1)}, u32[]{:S(2)}, u32[]{:S(2)}) collective-permute-start(f32[216,128]{1,0:T(8,128)S(1)} %get-tuple-element.139.up), channel_id=1, source_target_pairs={{8,0},{16,8},{24,16},{32,24},{40,32},{48,40},{56,48},{64,56},{72,6... | collective-permute-start | bytes 331784 | tf_op jit(solution)/shard_map/ppermute | solution.py:478

commit v3 on v2

--- a/solution.py
+++ b/solution.py
@@ -10,6 +10,7 @@
 LP = 56
 NX, NY = 64, 128
 LB = 10
+CHUNKS = LEVELS // LB
 HALO = 12
 LOW, HIGH = 0.7, 31.0
 MID, HALF = 0.5 * (HIGH + LOW), 0.5 * (HIGH - LOW)
@@ -34,40 +35,38 @@
 
 
 def interior_kernel(
-    scale, weight, lam, lam_next, theta, theta_next, vel_u, vel_v, mask, column,
-    stepped, sent, edge_rows, rhs, coupled, weights_out, flux,
+    scale, weight, lam_hbm, theta_hbm, u_hbm, v_hbm, mask, column,
+    stepped, sent, short, edge_rows, rhs, coupled, weights_out,
+    lam, theta, vel_u, vel_v, arrived,
 ):
-    step = pl.program_id(0)
+    def arrival(c, n):
+        source, target = ((lam_hbm, lam), (theta_hbm, theta), (u_hbm, vel_u), (v_hbm, vel_v))[n]
+        part = pl.ds(c * LB, LB)
+        return pltpu.make_async_copy(source.at[part], target.at[part], arrived.at[n, c])
+
+    for c in range(CHUNKS):
+        for n in range(4):
+            arrival(c, n).start()
     tile = (NX, NY)
     lane, row = lanes(tile), rows_of(tile)
     wet = mask[...].astype(F32)
-
-    @pl.when(step == 0)
-    def _():
-        sent[...] = jnp.zeros_like(sent)
-        edge_rows[...] = jnp.zeros_like(edge_rows)
-        rhs[...] = jnp.zeros_like(rhs)
-        flux[...] = jnp.zeros_like(flux)
-        weights_out[...] = jnp.zeros_like(weights_out)
-        coupled[...] = wet * column[...]
-
+    sent[...] = jnp.zeros_like(sent)
+    edge_rows[...] = jnp.zeros_like(edge_rows)
+    weights_out[...] = jnp.zeros_like(weights_out)
+    coupled[...] = wet * column[...]
     face_x = jnp.where(row == NX - 1, 0.0, wet * roll(wet, -1, 0))
     face_y = jnp.where(lane == NY - 1, 0.0, wet * roll(wet, -1, 1))
-    half = half_kappa(theta[0], scale[0, step * LB])
-    below = flux[...]
-    total = rhs[...]
-    for kk in range(LB):
-        k = step * LB + kk
+    for n in range(4):
+        arrival(0, n).wait()
+
+    def level(k, half, below, total):
+        after = jnp.minimum(k + 1, LEVELS - 1)
         w = weight[k]
-        here = lam[kk]
-        if kk + 1 < LB:
-            above = lam[kk + 1]
-            half_above = half_kappa(theta[kk + 1], scale[0, k + 1])
-        else:
-            above = lam_next[0]
-            half_above = half_kappa(theta_next[0], scale[0, jnp.minimum(k + 1, LEVELS - 1)])
-        half_u = vel_u[kk].astype(F32) * (0.5 * scale[1, k])
-        half_v = vel_v[kk].astype(F32) * (0.5 * scale[2, k])
+        here = lam[k]
+        above = lam[after]
+        half_above = half_kappa(theta[after], scale[0, after])
+        half_u = vel_u[k].astype(F32) * (0.5 * scale[1, k])
+        half_v = vel_v[k].astype(F32) * (0.5 * scale[2, k])
         dx = face_x * (roll(here, -1, 0) - here)
         sx = half + roll(half, -1, 0)
         dy = face_y * (roll(here, -1, 1) - here)
@@ -76,7 +75,7 @@
         value = here + dx * (sx + half_u) + roll(dx * (half_u - sx), 1, 0)
         value = value + dy * (sy + half_v) + roll(dy * (half_v - sy), 1, 1)
         value = wet * (value + (vertical - below))
-        stepped[kk] = value
+        stepped[k] = value
         total = total + w * value
         at = 16 + 2 * k
         pair = (lane == at) | (lane == at + 1)
@@ -94,21 +93,32 @@
         weights_out[LP : LP + 8, :] = jnp.where(
             (lane8 == at) | (lane8 == at + 1), w, weights_out[LP : LP + 8, :]
         )
-        below, half = vertical, half_above
-    flux[...] = below
+        return half_above, vertical, total
+
+    def chunk(c, carry):
+        @pl.when(c + 1 < CHUNKS)
+        def _():
+            for n in range(4):
+                arrival(c + 1, n).wait()
+
+        for kk in range(LB):
+            carry = level(c * LB + kk, *carry)
+        return carry
+
+    zero = jnp.zeros(tile, F32)
+    total = lax.fori_loop(0, CHUNKS, chunk, (half_kappa(theta[0], scale[0, 0]), zero, zero))[2]
     rhs[...] = total
-
-    @pl.when(step == LEVELS // LB - 1)
-    def _():
-        rim = (lane < HALO) | (lane >= NY - HALO)
-        sent[0:64] = jnp.where(rim, total, sent[0:64])
-        sent[64:128] = jnp.where(rim, coupled[...], sent[64:128])
-        lane_e = lanes((LP, NY))
-        packed = jnp.where((lane_e < HALO) | (lane_e >= NY - HALO), edge_rows[0], 0.0)
-        for m in range(1, 5):
-            inside = (lane_e >= 24 * m - HALO) & (lane_e < 24 * m + HALO)
-            packed = jnp.where(inside, roll(edge_rows[m], 24 * m, 1), packed)
-        sent[192 : 192 + LP] = packed
+    rim = (lane < HALO) | (lane >= NY - HALO)
+    sent[0:64] = jnp.where(rim, total, sent[0:64])
+    sent[64:128] = jnp.where(rim, coupled[...], sent[64:128])
+    lane_e = lanes((LP, NY))
+    packed = jnp.where((lane_e < HALO) | (lane_e >= NY - HALO), edge_rows[0], 0.0)
+    for m in range(1, 5):
+        inside = (lane_e >= 24 * m - HALO) & (lane_e < 24 * m + HALO)
+        packed = jnp.where(inside, roll(edge_rows[m], 24 * m, 1), packed)
+    sent[192 : 192 + LP] = packed
+    short[0:128] = sent[0:128]
+    short[128 : 128 + LP] = packed
 
 
 def column_kernel(
@@ -161,7 +171,7 @@
     north = (lane_e >= 0) & (lane_e < HALO)
     for m in range(1, 5):
         north = north | ((lane_e >= 24 * m) & (lane_e < 24 * m + HALO))
-    levels_outer = jnp.where(north, from_north[192 : 192 + LP], from_south[192 : 192 + LP])
+    levels_outer = jnp.where(north, from_north[128 : 128 + LP], from_south[192 : 192 + LP])
     strip_lane = lanes((16, NY))
     window = (strip_lane >= HALO) & (strip_lane < 3 * HALO)
 
@@ -303,77 +313,80 @@
 
 def solve_kernel(
     weight, gathered, basis, stepped, edges_y, edges_x, mask,
-    out, surface, flag, scaled,
+    out, surface, flag, values, left,
 ):
-    step = pl.program_id(0)
-
-    @pl.when(step == 0)
-    def _():
-        line = jnp.sum(gathered[...], axis=0, keepdims=True)
-        shape = (32, NY)
-        column = jnp.sum(jnp.where(lanes(shape) == rows_of(shape), line, 0.0), axis=1, keepdims=True)
-        d = jnp.broadcast_to(column, shape)[0:24]
-        d0 = d[0:1]
-        d = d / d0
-        row = rows_of((24, NY))
-        moment = jnp.where((row & 1) == 0, 2.0 * d - 1.0, 2.0 * d - d[1:2])
-        moment = jnp.where(row < 2, d, moment)
-        largest = jnp.maximum(jnp.max(jnp.abs(moment), axis=0, keepdims=True), 1.0)
-        quarter = 0.5 * HALF
-        row16 = rows_of((16, NY))
-        r, p = moment, moment
-        rc = jnp.where(row16 == 0, 1.0, 0.0)
-        pc = rc
-        xc = jnp.zeros((16, NY), F32)
-        rr = jnp.ones((1, NY), F32)
-        worst = jnp.ones((1, NY), F32)
-        good = jnp.ones((1, NY), F32)
-        for n in range(ITERS):
-            shifted = jnp.where(row == 0, p[1:2], roll(p, 1, 0)) + roll(p, -1, 0)
-            hp = MID * p + quarter * shifted
-            alpha = r[n : n + 1] / hp[n : n + 1]
-            good = jnp.where(alpha > 0.0, good, 0.0)
-            xc = xc + alpha * pc
-            if n == ITERS - 1:
-                break
-            fresh = r - alpha * hp
-            lead = -alpha * (quarter * (2.0 if n == 0 else 1.0))
-            beta = lead * fresh[n + 1 : n + 2] / r[n : n + 1]
-            image = MID * pc + quarter * (
-                roll(pc, 1, 0)
-                + jnp.where(row16 == 1, pc[0:1], 0.0)
-                + jnp.where(row16 == 15, 0.0, roll(pc, -1, 0))
-            )
-            rc = rc - alpha * image
-            pc = rc + beta * pc
-            p = fresh + beta * p
-            r = fresh
-            rr = rr * beta
-            good = jnp.where(rr > 0.0, good, 0.0)
-            size = jnp.sum(jnp.abs(rc), axis=0, keepdims=True)
-            worst = jnp.maximum(worst, size * size / rr)
-        good = jnp.where(worst * largest < GUARD, good, 0.0)
-        x = jnp.zeros((NX, NY), F32)
-        for n in range(ITERS):
-            x = x + xc[n : n + 1] * basis[n]
-        x = jnp.where(good > 0.0, x, 0.0)
-        surface[...] = x
-        scaled[...] = mask[...].astype(F32) * x
-        flag[0] = jnp.min(good).astype(jnp.int32)
+    line = jnp.sum(gathered[...], axis=0, keepdims=True)
+    shape = (32, NY)
+    column = jnp.sum(jnp.where(lanes(shape) == rows_of(shape), line, 0.0), axis=1, keepdims=True)
+    d = jnp.broadcast_to(column, shape)[0:24]
+    d0 = d[0:1]
+    d = d / d0
+    row = rows_of((24, NY))
+    moment = jnp.where((row & 1) == 0, 2.0 * d - 1.0, 2.0 * d - d[1:2])
+    moment = jnp.where(row < 2, d, moment)
+    largest = jnp.maximum(jnp.max(jnp.abs(moment), axis=0, keepdims=True), 1.0)
+    quarter = 0.5 * HALF
+    row16 = rows_of((16, NY))
+    r, p = moment, moment
+    rc = jnp.where(row16 == 0, 1.0, 0.0)
+    pc = rc
+    xc = jnp.zeros((16, NY), F32)
+    rr = jnp.ones((1, NY), F32)
+    worst = jnp.ones((1, NY), F32)
+    good = jnp.ones((1, NY), F32)
+    for n in range(ITERS):
+        shifted = jnp.where(row == 0, p[1:2], roll(p, 1, 0)) + roll(p, -1, 0)
+        hp = MID * p + quarter * shifted
+        alpha = r[n : n + 1] / hp[n : n + 1]
+        good = jnp.where(alpha > 0.0, good, 0.0)
+        xc = xc + alpha * pc
+        if n == ITERS - 1:
+            break
+        fresh = r - alpha * hp
+        lead = -alpha * (quarter * (2.0 if n == 0 else 1.0))
+        beta = lead * fresh[n + 1 : n + 2] / r[n : n + 1]
+        image = MID * pc + quarter * (
+            roll(pc, 1, 0)
+            + jnp.where(row16 == 1, pc[0:1], 0.0)
+            + jnp.where(row16 == 15, 0.0, roll(pc, -1, 0))
+        )
+        rc = rc - alpha * image
+        pc = rc + beta * pc
+        p = fresh + beta * p
+        r = fresh
+        rr = rr * beta
+        good = jnp.where(rr > 0.0, good, 0.0)
+        size = jnp.sum(jnp.abs(rc), axis=0, keepdims=True)
+        worst = jnp.maximum(worst, size * size / rr)
+    good = jnp.where(worst * largest < GUARD, good, 0.0)
+    x = jnp.zeros((NX, NY), F32)
+    for n in range(ITERS):
+        x = x + xc[n : n + 1] * basis[n]
+    x = jnp.where(good > 0.0, x, 0.0)
+    surface[...] = x
+    wx = mask[...].astype(F32) * x
+    flag[0] = jnp.min(good).astype(jnp.int32)
 
     lane = lanes((NX, NY))
-    wx = scaled[...]
-    for kk in range(LB):
-        k = step * LB + kk
-        shifted = pltpu.roll(edges_y[...], 111 + 128 - 2 * k, 1)
-        value = stepped[kk] - weight[k] * wx
-        out[kk] = value + jnp.where((lane == 0) | (lane == NY - 1), shifted, 0.0)
-        out[kk, 0:1, :] += edges_x[pl.ds(k, 1), :]
-        out[kk, NX - 1 : NX, :] += edges_x[pl.ds(LP + k, 1), :]
-
-
-def whole(shape):
-    return pl.BlockSpec(shape, lambda *_: (0,) * len(shape))
+    rim = (lane == 0) | (lane == NY - 1)
+
+    def departure(c):
+        part = pl.ds(c * LB, LB)
+        return pltpu.make_async_copy(values.at[part], out.at[part], left.at[c])
+
+    def chunk(c, carry):
+        for kk in range(LB):
+            k = c * LB + kk
+            shifted = pltpu.roll(edges_y[...], 111 + 128 - 2 * k, 1)
+            values[k] = stepped[k] - weight[k] * wx + jnp.where(rim, shifted, 0.0)
+            values[k, 0:1, :] += edges_x[pl.ds(k, 1), :]
+            values[k, NX - 1 : NX, :] += edges_x[pl.ds(LP + k, 1), :]
+        departure(c).start()
+        return carry
+
+    lax.fori_loop(0, CHUNKS, chunk, 0)
+    for c in range(CHUNKS):
+        departure(c).wait()
 
 
 def arrays(*shapes):
@@ -431,30 +444,33 @@
 def on_device(
     adjoint_in, state_theta, state_u, state_v, level_scale, land_mask, level_weights, column_weight
 ):
-    steps = LEVELS // LB
     smem = pl.BlockSpec(memory_space=pltpu.SMEM)
-    block = pl.BlockSpec((LB, NX, NY), lambda i: (i, 0, 0))
-    following = pl.BlockSpec(
-        (1, NX, NY), lambda i: (jnp.minimum((i + 1) * LB, LEVELS - 1), 0, 0)
+    hbm = pl.BlockSpec(memory_space=pltpu.HBM)
+    tile = (NX, NY)
+    adjoint_in, state_theta, state_u, state_v, level_scale, kernel_weights = (
+        pltpu.with_memory_space_constraint(x, pltpu.HBM)
+        for x in (
+            adjoint_in, state_theta, state_u, state_v, level_scale, level_weights
+        )
     )
-    tile = (NX, NY)
-    adjoint_in, state_theta, state_u, state_v = (
-        pltpu.with_memory_space_constraint(x, pltpu.HBM)
-        for x in (adjoint_in, state_theta, state_u, state_v)
-    )
-    stepped, sent, edge_rows, rhs, coupled, weights = pl.pallas_call(
+    stepped, sent, short, edge_rows, rhs, coupled, weights = pl.pallas_call(
         interior_kernel,
         name="interior",
-        grid=(steps,),
-        in_specs=[smem, smem, block, following, block, following, block, block] + on_chip(2),
-        out_specs=[block] + on_chip(5),
+        in_specs=[smem] * 2 + [hbm] * 4 + on_chip(2),
+        out_specs=on_chip(7),
         out_shape=arrays(
-            (LEVELS, NX, NY), (192 + LP, NY), (5, LP, NY), tile, tile, (LP + 8, NY)
+            (LEVELS, NX, NY), (192 + LP, NY), (128 + LP, NY), (5, LP, NY), tile, tile, (LP + 8, NY)
         ),
-        scratch_shapes=[pltpu.VMEM(tile, F32)],
+        scratch_shapes=[
+            pltpu.VMEM((LEVELS, NX, NY), F32),
+            pltpu.VMEM((LEVELS, NX, NY), jnp.bfloat16),
+            pltpu.VMEM((LEVELS, NX, NY), jnp.bfloat16),
+            pltpu.VMEM((LEVELS, NX, NY), jnp.bfloat16),
+            pltpu.SemaphoreType.DMA((4, CHUNKS)),
+        ],
         compiler_params=limit(16),
     )(
-        level_scale, level_weights, adjoint_in, adjoint_in, state_theta, state_theta,
+        level_scale, kernel_weights, adjoint_in, state_theta,
         state_u, state_v, land_mask, column_weight,
     )
 
@@ -464,7 +480,7 @@
 
     onward, back = ring("ty")
     from_south = lax.ppermute(sent, "ty", onward)
-    from_north = lax.ppermute(sent, "ty", back)
+    from_north = lax.ppermute(short, "ty", back)
     down, up, rhs, outer, edges_y = pl.pallas_call(
         column_kernel,
         name="columns",
@@ -490,17 +506,16 @@
     out, surface, flag = pl.pallas_call(
         solve_kernel,
         name="solve",
-        grid=(steps,),
-        in_specs=[smem] + on_chip(2) + [block] + on_chip(3),
-        out_specs=[block] + on_chip(1) + [smem],
+        in_specs=[smem] + on_chip(6),
+        out_specs=[hbm] + on_chip(1) + [smem],
         out_shape=(
             pltpu.HBM((LEVELS, NX, NY), F32),
             jax.ShapeDtypeStruct(tile, F32),
             jax.ShapeDtypeStruct((1,), jnp.int32),
         ),
-        scratch_shapes=[pltpu.VMEM(tile, F32)],
+        scratch_shapes=[pltpu.VMEM((LEVELS, NX, NY), F32), pltpu.SemaphoreType.DMA((CHUNKS,))],
         compiler_params=limit(8),
-    )(level_weights, gathered, basis, stepped, edges_y, edges_x, land_mask)
+    )(kernel_weights, gathered, basis, stepped, edges_y, edges_x, land_mask)
 
     def unsolved(carry):
         return carry[0] == 0

time: 49 us -> 48.5 us (0.990)
  blocking collectives: 20.9 us -> 18 us
  waiting for transfers between devices: 5.13 us -> 7.66 us
  local copies, waits for them, and re-layouts: 0.69 us -> 0.02 us
    all_to_all x1, blocking collectives: 20.9 us -> 18 us  [on_device(): gathered = lax.all_to_all(dots, ('tx', 'ty'), 0, 0, tiled=True)]
    ppermute x1, waiting for transfers between devices: 2.58 us -> 4.17 us  [on_device(): from_north = lax.ppermute(short, 'ty', back)]
    ppermute x1, starting transfers between devices: 1.43 us -> 0.01 us  [on_device(): from_north = lax.ppermute(short, 'ty', back)]
    ppermute x1, starting transfers between devices: 1.63 us -> 3.04 us  [on_device(): from_south = lax.ppermute(sent, 'ty', onward)]
    ppermute x1, waiting for transfers between devices: 0.61 us -> 1.51 us  [on_device(): from_up = lax.ppermute(down, 'tx', onward)]
    unnamed x8 -> x6, local copies, waits for them, and re-layouts: 0.69 us -> 0.02 us
  transfers between devices with their start and end apart: 4 -> 4, of which waited for: 4 -> 3; matrix products, arithmetic and copies ran while one was open for 0% -> 0% of each run, Pallas kernels for 0% -> 0%
where the time goes in v3:
time: 48.5 us; the launch traced here: 48.3 us
  blocking collectives  18 us (37%)
  Pallas kernels  13.1 us (27%)
  starting transfers between devices  8.12 us (17%)
  waiting for transfers between devices  7.66 us (16%)
  between operations  0.7 us (1%)
  loops' own time  0.64 us (1%)
    all_to_all x1, blocking collectives, on_device(): gathered = lax.all_to_all(dots, ('tx', 'ty'), 0, 0, tiled=True)  18 us
    pallas_call x1, Pallas kernels, on_device(): pl.pallas_call(interior_kernel, name='interior', in_specs=[smem] * 2 + [h...  8.09 us
    ppermute x1, waiting for transfers between devices, on_device(): from_north = lax.ppermute(short, 'ty', back)  4.17 us
    ppermute x1, starting transfers between devices, on_device(): from_down = lax.ppermute(up, 'tx', back)  3.8 us
    pallas_call x1, Pallas kernels, on_device(): pl.pallas_call(solve_kernel, name='solve', in_specs=[smem] + on_chip(6),...  3.37 us
    ppermute x1, starting transfers between devices, on_device(): from_south = lax.ppermute(sent, 'ty', onward)  3.04 us
    ppermute x1, waiting for transfers between devices, on_device(): from_down = lax.ppermute(up, 'tx', back)  1.98 us
    ppermute x1, waiting for transfers between devices, on_device(): from_up = lax.ppermute(down, 'tx', onward)  1.51 us
  transfers between devices with their start and end apart: 4, of which 3 were waited for; matrix products, arithmetic and copies ran while one was open for 0% of the time, Pallas kernels for 0%

profile of v3, /device:TPU:1, one launch (start us, length us, event | category | flops | bytes accessed | tf_op | source)
XLA Modules:
  0.0 48.3 jit_solution(16402695184914929611)
XLA Ops:
  0.6 0.0 copy-start.4
  0.6 8.1 %interior.1 = (f32[50,64,128]{2,1,0:T(8,128)S(1)}, f32[248,128]{1,0:T(8,128)S(1)}, f32[184,128]{1,0:T(8,128)S(1)}, f32[5,56,128]{2,1,0:T(8,128)S(1)}, f32[64,128...) custom-call(f32[3,50]{1,0:T(4,128)} %scale.1, f32[50]{0:T(128)} %weight.3, f32[50,64,128]{2,1,0:T(8,128)} %lam_hbm.1, ...), custom_call_target="tpu_custom_call" | custom-call | tf_op jit(solution)/shard_map/interior/pallas_call | solution.py:456
  8.7 3.0 %collective-permute-start.8 = (f32[248,128]{1,0:T(8,128)S(1)}, f32[248,128]{1,0:T(8,128)S(1)}, u32[]{:S(2)}, u32[]{:S(2)}) collective-permute-start(f32[248,128]{1,0:T(8,128)S(1)} %get-tuple-element.134.sent), channel_id=1, source_target_pairs={{0,1},{1,2},{2,3},{3,4},{4,5},{5,6},{6,7},{7,0},{8,9},{9,10},{10,1... | collective-permute-start | bytes 380936 | tf_op jit(solution)/shard_map/ppermute | solution.py:482
  11.8 0.0 collective-permute-start.9
  11.8 4.2 %collective-permute-done.9.from_north = f32[184,128]{1,0:T(8,128)S(1)} collective-permute-done((f32[184,128]{1,0:T(8,128)S(1)}, f32[184,128]{1,0:T(8,128)S(1)}, u32[]{:S(2)}, u32[]{:S(2)}) %collective-permute-start.9) | collective-permute-done | bytes 94240 | tf_op jit(solution)/shard_map/ppermute | solution.py:483
  15.9 0.0 collective-permute-done.8.from_south
  15.9 0.3 columns.1
  16.2 0.0 copy-start.3
  16.2 0.0 copy-start.5
  16.3 1.3 %collective-permute-start.10 = (f32[272,128]{1,0:T(8,128)S(1)}, f32[272,128]{1,0:T(8,128)S(1)}, u32[]{:S(2)}, u32[]{:S(2)}) collective-permute-start(f32[272,128]{1,0:T(8,128)S(1)} %get-tuple-element.140.down), channel_id=1, source_target_pairs={{0,8},{8,16},{16,24},{24,32},{32,40},{40,48},{48,56},{56,64},{64,7... | collective-permute-start | bytes 417800 | tf_op jit(solution)/shard_map/ppermute | solution.py:493
  17.5 3.8 %collective-permute-start.11 = (f32[216,128]{1,0:T(8,128)S(1)}, f32[216,128]{1,0:T(8,128)S(1)}, u32[]{:S(2)}, u32[]{:S(2)}) collective-permute-start(f32[216,128]{1,0:T(8,128)S(1)} %get-tuple-element.141.up), channel_id=1, source_target_pairs={{8,0},{16,8},{24,16},{32,24},{40,32},{48,40},{56,48},{64,56},{72,6... | collective-permute-start | bytes 331784 | tf_op jit(solution)/shard_map/ppermute | solution.py:494
  21.3 2.0 %collective-permute-done.11.from_down = f32[216,128]{1,0:T(8,128)S(1)} collective-permute-done((f32[216,128]{1,0:T(8,128)S(1)}, f32[216,128]{1,0:T(8,128)S(1)}, u32[]{:S(2)}, u32[]{:S(2)}) %collective-permute-start.11) | collective-permute-done | bytes 110624 | tf_op jit(solution)/shard_map/ppermute | solution.py:494
  23.3 1.5 %collective-permute-done.10.from_up = f32[272,128]{1,0:T(8,128)S(1)} collective-permute-done((f32[272,128]{1,0:T(8,128)S(1)}, f32[272,128]{1,0:T(8,128)S(1)}, u32[]{:S(2)}, u32[]{:S(2)}) %collective-permute-start.10) | collective-permute-done | bytes 139296 | tf_op jit(solution)/shard_map/ppermute | solution.py:493
  24.8 1.4 %basis.1 = (f32[12,64,128]{2,1,0:T(8,128)S(1)}, f32[128,128]{1,0:T(8,128)S(1)}, f32[112,128]{1,0:T(8,128)S(1)}, f32[64,128]{1,0:T(8,128)S(1)}) custom-call(f32[272,128]{1,0:T(8,128)S(1)} %collective-permute-done.10.from_up, f32[216,128]{1,0:T(8,128)S(1)} %collective-permute-done.11.from_down, f32[272,128]{1,0:T(8,128)S(1)} %get-tuple-element.140.down, ...), custom_call_target="tpu_custom_call" | custom-call | tf_op jit(solution)/shard_map/basis/pallas_call | solution.py:496
  26.2 18.0 %all_to_all.11 = f32[128,1,128]{2,1,0:T(1,128)S(1)} all-to-all(f32[128,1,128]{2,1,0:T(1,128)S(1)} %bitcast.6), channel_id=1, replica_groups=mesh['tx'=16,'ty'=8] {'tx','ty'}, dimensions={0} | all-to-all | bytes 131072 | tf_op jit(solution)/shard_map/all_to_all | solution.py:505
  44.3 0.0 copy-done.4
  44.3 3.4 %solve.1 = (f32[50,64,128]{2,1,0:T(8,128)}, f32[64,128]{1,0:T(8,128)}, s32[1]{0:T(128)}) custom-call(f32[50]{0:T(128)} %weight.3, f32[128,128]{1,0:T(8,128)S(1)} %bitcast.5, f32[12,64,128]{2,1,0:T(8,128)S(1)} %get-tuple-element.145.basis, f32[50,64,128]{2,1,0:T(8,128)S(1)} %get-tuple-element.146.stepped, f32[64,128]{1,0:T(8,128)S(1)} %get-tuple-element.147.edges_y, ...), custom_call_target="tpu_custom_call" | custom-call | tf_op jit(solution)/shard_map/solve/pallas_call | solution.py:506
  47.6 0.0 copy-done.3
  47.6 0.0 copy-done.5
  47.7 0.6 %while.28 = (s32[]{:T(128)}, f32[50,64,128]{2,1,0:T(8,128)}, f32[64,128]{1,0:T(8,128)}, f32[50]{0:T(128)S(1)}, s32[64,128]{1,0:T(8,128)S(1)}, /*index=5*/f32[64,...) while((s32[]{:T(128)}, f32[50,64,128]{2,1,0:T(8,128)}, f32[64,128]{1,0:T(8,128)}, f32[50]{0:T(128)S(1)}, ...), condition=%region_9.0_spmd, body=%region_0.0_spmd | while | flops 1262598 | bytes 17688772 | solution.py:529
Async XLA Ops:
  0.6 43.6 %copy-start.4 = (s32[64,128]{1,0:T(8,128)S(1)}, s32[64,128]{1,0:T(8,128)}, u32[]{:S(2)}) copy-start(s32[64,128]{1,0:T(8,128)} %mask.3) | copy-start | bytes 98308
  8.7 7.2 %collective-permute-start.8 = (f32[248,128]{1,0:T(8,128)S(1)}, f32[248,128]{1,0:T(8,128)S(1)}, u32[]{:S(2)}, u32[]{:S(2)}) collective-permute-start(f32[248,128]{1,0:T(8,128)S(1)} %get-tuple-element.134.sent), channel_id=1, source_target_pairs={{0,1},{1,2},{2,3},{3,4},{4,5},{5,6},{6,7},{7,0},{8,9},{9,10},{10,1... | collective-permute-start | bytes 380936 | tf_op jit(solution)/shard_map/ppermute | solution.py:482
  11.8 4.2 %collective-permute-start.9 = (f32[184,128]{1,0:T(8,128)S(1)}, f32[184,128]{1,0:T(8,128)S(1)}, u32[]{:S(2)}, u32[]{:S(2)}) collective-permute-start(f32[184,128]{1,0:T(8,128)S(1)} %get-tuple-element.135), channel_id=1, source_target_pairs={{1,0},{2,1},{3,2},{4,3},{5,4},{6,5},{7,6},{0,7},{9,8},{10,9},{11,1... | collective-permute-start | bytes 282632 | tf_op jit(solution)/shard_map/ppermute | solution.py:483
  16.2 31.4 %copy-start.3 = (f32[64,128]{1,0:T(8,128)S(1)}, f32[64,128]{1,0:T(8,128)}, u32[]{:S(2)}) copy-start(f32[64,128]{1,0:T(8,128)} %column.1) | copy-start | bytes 98308
  16.2 31.4 %copy-start.5 = (f32[50]{0:T(128)S(1)}, f32[50]{0:T(128)}, u32[]{:S(2)}) copy-start(f32[50]{0:T(128)} %weight.3) | copy-start | bytes 604
  16.3 8.6 %collective-permute-start.10 = (f32[272,128]{1,0:T(8,128)S(1)}, f32[272,128]{1,0:T(8,128)S(1)}, u32[]{:S(2)}, u32[]{:S(2)}) collective-permute-start(f32[272,128]{1,0:T(8,128)S(1)} %get-tuple-element.140.down), channel_id=1, source_target_pairs={{0,8},{8,16},{16,24},{24,32},{32,40},{40,48},{48,56},{56,64},{64,7... | collective-permute-start | bytes 417800 | tf_op jit(solution)/shard_map/ppermute | solution.py:493
  17.5 5.8 %collective-permute-start.11 = (f32[216,128]{1,0:T(8,128)S(1)}, f32[216,128]{1,0:T(8,128)S(1)}, u32[]{:S(2)}, u32[]{:S(2)}) collective-permute-start(f32[216,128]{1,0:T(8,128)S(1)} %get-tuple-element.141.up), channel_id=1, source_target_pairs={{8,0},{16,8},{24,16},{32,24},{40,32},{48,40},{56,48},{64,56},{72,6... | collective-permute-start | bytes 331784 | tf_op jit(solution)/shard_map/ppermute | solution.py:494

commit v4 on v3

--- a/solution.py
+++ b/solution.py
@@ -37,7 +37,7 @@
 def interior_kernel(
     scale, weight, lam_hbm, theta_hbm, u_hbm, v_hbm, mask, column,
     stepped, sent, short, edge_rows, rhs, coupled, weights_out,
-    lam, theta, vel_u, vel_v, arrived,
+    lam, theta, vel_u, vel_v, kept, arrived,
 ):
     def arrival(c, n):
         source, target = ((lam_hbm, lam), (theta_hbm, theta), (u_hbm, vel_u), (v_hbm, vel_v))[n]
@@ -77,22 +77,13 @@
         value = wet * (value + (vertical - below))
         stepped[k] = value
         total = total + w * value
-        at = 16 + 2 * k
-        pair = (lane == at) | (lane == at + 1)
-        shift = at + 1
-        sent[0:64] = jnp.where(pair, pltpu.roll(here, shift, 1), sent[0:64])
-        sent[64:128] = jnp.where(pair, pltpu.roll(half, shift, 1), sent[64:128])
-        sent[128:192] = jnp.where(lane == at, pltpu.roll(half_v, shift, 1), sent[128:192])
+        kept[k] = half
         edge_rows[0, pl.ds(k, 1), :] = here[NX - 1 :]
         edge_rows[1, pl.ds(k, 1), :] = half[NX - 1 :]
         edge_rows[2, pl.ds(k, 1), :] = half_u[NX - 1 :]
         edge_rows[3, pl.ds(k, 1), :] = here[:1]
         edge_rows[4, pl.ds(k, 1), :] = half[:1]
         weights_out[pl.ds(k, 1), :] = jnp.full((1, NY), w, F32)
-        lane8 = lanes((8, NY))
-        weights_out[LP : LP + 8, :] = jnp.where(
-            (lane8 == at) | (lane8 == at + 1), w, weights_out[LP : LP + 8, :]
-        )
         return half_above, vertical, total
 
     def chunk(c, carry):
@@ -108,6 +99,28 @@
     zero = jnp.zeros(tile, F32)
     total = lax.fori_loop(0, CHUNKS, chunk, (half_kappa(theta[0], scale[0, 0]), zero, zero))[2]
     rhs[...] = total
+
+    def pack(c, packs):
+        for kk in range(LB):
+            k = c * LB + kk
+            at = 16 + 2 * k
+            pair = (lane == at) | (lane == at + 1)
+            half_v = vel_v[k].astype(F32) * (0.5 * scale[2, k])
+            packs = (
+                jnp.where(pair, pltpu.roll(lam[k], at + 1, 1), packs[0]),
+                jnp.where(pair, pltpu.roll(kept[k], at + 1, 1), packs[1]),
+                jnp.where(lane == at, pltpu.roll(half_v, at + 1, 1), packs[2]),
+            )
+        return packs
+
+    packs = lax.fori_loop(0, CHUNKS, pack, (zero, zero, zero))
+    for n in range(3):
+        sent[64 * n : 64 * n + 64] = packs[n]
+    lane_w, row_w = lanes((LP, NY)), rows_of((LP, NY))
+    at_level = (lane_w == 16 + 2 * row_w) | (lane_w == 17 + 2 * row_w)
+    weights_out[LP:] = jnp.broadcast_to(
+        jnp.sum(jnp.where(at_level, weights_out[0:LP], 0.0), axis=0, keepdims=True), (8, NY)
+    )
     rim = (lane < HALO) | (lane >= NY - HALO)
     sent[0:64] = jnp.where(rim, total, sent[0:64])
     sent[64:128] = jnp.where(rim, coupled[...], sent[64:128])
@@ -466,6 +479,7 @@
             pltpu.VMEM((LEVELS, NX, NY), jnp.bfloat16),
             pltpu.VMEM((LEVELS, NX, NY), jnp.bfloat16),
             pltpu.VMEM((LEVELS, NX, NY), jnp.bfloat16),
+            pltpu.VMEM((LEVELS, NX, NY), F32),
             pltpu.SemaphoreType.DMA((4, CHUNKS)),
         ],
         compiler_params=limit(16),

time: 48.5 us -> 47.9 us (0.988)
  Pallas kernels: 13.1 us -> 12.5 us
    pallas_call x1, Pallas kernels: 8.09 us -> 7.49 us  [on_device(): pl.pallas_call(interior_kernel, name='interior', in_specs=[smem] * 2 + [h...]
where the time goes in v4:
time: 47.9 us; the launch traced here: 47.7 us
  blocking collectives  18 us (38%)
  Pallas kernels  12.5 us (26%)
  starting transfers between devices  8.12 us (17%)
  waiting for transfers between devices  7.66 us (16%)
  between operations  0.7 us (1%)
  loops' own time  0.64 us (1%)
    all_to_all x1, blocking collectives, on_device(): gathered = lax.all_to_all(dots, ('tx', 'ty'), 0, 0, tiled=True)  18 us
    pallas_call x1, Pallas kernels, on_device(): pl.pallas_call(interior_kernel, name='interior', in_specs=[smem] * 2 + [h...  7.49 us
    ppermute x1, waiting for transfers between devices, on_device(): from_north = lax.ppermute(short, 'ty', back)  4.17 us
    ppermute x1, starting transfers between devices, on_device(): from_down = lax.ppermute(up, 'tx', back)  3.8 us
    pallas_call x1, Pallas kernels, on_device(): pl.pallas_call(solve_kernel, name='solve', in_specs=[smem] + on_chip(6),...  3.37 us
    ppermute x1, starting transfers between devices, on_device(): from_south = lax.ppermute(sent, 'ty', onward)  3.04 us
    ppermute x1, waiting for transfers between devices, on_device(): from_down = lax.ppermute(up, 'tx', back)  1.98 us
    ppermute x1, waiting for transfers between devices, on_device(): from_up = lax.ppermute(down, 'tx', onward)  1.51 us
  transfers between devices with their start and end apart: 4, of which 3 were waited for; matrix products, arithmetic and copies ran while one was open for 0% of the time, Pallas kernels for 0%

profile of v4, /device:TPU:1, one launch (start us, length us, event | category | flops | bytes accessed | tf_op | source)
XLA Modules:
  0.0 47.7 jit_solution(11261056844888816069)
XLA Ops:
  0.6 0.0 copy-start.4
  0.6 7.5 %interior.1 = (f32[50,64,128]{2,1,0:T(8,128)S(1)}, f32[248,128]{1,0:T(8,128)S(1)}, f32[184,128]{1,0:T(8,128)S(1)}, f32[5,56,128]{2,1,0:T(8,128)S(1)}, f32[64,128...) custom-call(f32[3,50]{1,0:T(4,128)} %scale.1, f32[50]{0:T(128)} %weight.3, f32[50,64,128]{2,1,0:T(8,128)} %lam_hbm.1, ...), custom_call_target="tpu_custom_call" | custom-call | tf_op jit(solution)/shard_map/interior/pallas_call | solution.py:469
  8.1 3.0 %collective-permute-start.8 = (f32[248,128]{1,0:T(8,128)S(1)}, f32[248,128]{1,0:T(8,128)S(1)}, u32[]{:S(2)}, u32[]{:S(2)}) collective-permute-start(f32[248,128]{1,0:T(8,128)S(1)} %get-tuple-element.134.sent), channel_id=1, source_target_pairs={{0,1},{1,2},{2,3},{3,4},{4,5},{5,6},{6,7},{7,0},{8,9},{9,10},{10,1... | collective-permute-start | bytes 380936 | tf_op jit(solution)/shard_map/ppermute | solution.py:496
  11.2 0.0 collective-permute-start.9
  11.2 4.2 %collective-permute-done.9.from_north = f32[184,128]{1,0:T(8,128)S(1)} collective-permute-done((f32[184,128]{1,0:T(8,128)S(1)}, f32[184,128]{1,0:T(8,128)S(1)}, u32[]{:S(2)}, u32[]{:S(2)}) %collective-permute-start.9) | collective-permute-done | bytes 94240 | tf_op jit(solution)/shard_map/ppermute | solution.py:497
  15.4 0.0 collective-permute-done.8.from_south
  15.4 0.3 columns.1
  15.6 0.0 copy-start.3
  15.7 0.0 copy-start.5
  15.7 1.3 %collective-permute-start.10 = (f32[272,128]{1,0:T(8,128)S(1)}, f32[272,128]{1,0:T(8,128)S(1)}, u32[]{:S(2)}, u32[]{:S(2)}) collective-permute-start(f32[272,128]{1,0:T(8,128)S(1)} %get-tuple-element.140.down), channel_id=1, source_target_pairs={{0,8},{8,16},{16,24},{24,32},{32,40},{40,48},{48,56},{56,64},{64,7... | collective-permute-start | bytes 417800 | tf_op jit(solution)/shard_map/ppermute | solution.py:507
  16.9 3.8 %collective-permute-start.11 = (f32[216,128]{1,0:T(8,128)S(1)}, f32[216,128]{1,0:T(8,128)S(1)}, u32[]{:S(2)}, u32[]{:S(2)}) collective-permute-start(f32[216,128]{1,0:T(8,128)S(1)} %get-tuple-element.141.up), channel_id=1, source_target_pairs={{8,0},{16,8},{24,16},{32,24},{40,32},{48,40},{56,48},{64,56},{72,6... | collective-permute-start | bytes 331784 | tf_op jit(solution)/shard_map/ppermute | solution.py:508
  20.7 2.0 %collective-permute-done.11.from_down = f32[216,128]{1,0:T(8,128)S(1)} collective-permute-done((f32[216,128]{1,0:T(8,128)S(1)}, f32[216,128]{1,0:T(8,128)S(1)}, u32[]{:S(2)}, u32[]{:S(2)}) %collective-permute-start.11) | collective-permute-done | bytes 110624 | tf_op jit(solution)/shard_map/ppermute | solution.py:508
  22.7 1.5 %collective-permute-done.10.from_up = f32[272,128]{1,0:T(8,128)S(1)} collective-permute-done((f32[272,128]{1,0:T(8,128)S(1)}, f32[272,128]{1,0:T(8,128)S(1)}, u32[]{:S(2)}, u32[]{:S(2)}) %collective-permute-start.10) | collective-permute-done | bytes 139296 | tf_op jit(solution)/shard_map/ppermute | solution.py:507
  24.2 1.4 %basis.1 = (f32[12,64,128]{2,1,0:T(8,128)S(1)}, f32[128,128]{1,0:T(8,128)S(1)}, f32[112,128]{1,0:T(8,128)S(1)}, f32[64,128]{1,0:T(8,128)S(1)}) custom-call(f32[272,128]{1,0:T(8,128)S(1)} %collective-permute-done.10.from_up, f32[216,128]{1,0:T(8,128)S(1)} %collective-permute-done.11.from_down, f32[272,128]{1,0:T(8,128)S(1)} %get-tuple-element.140.down, ...), custom_call_target="tpu_custom_call" | custom-call | tf_op jit(solution)/shard_map/basis/pallas_call | solution.py:510
  25.6 18.0 %all_to_all.11 = f32[128,1,128]{2,1,0:T(1,128)S(1)} all-to-all(f32[128,1,128]{2,1,0:T(1,128)S(1)} %bitcast.6), channel_id=1, replica_groups=mesh['tx'=16,'ty'=8] {'tx','ty'}, dimensions={0} | all-to-all | bytes 131072 | tf_op jit(solution)/shard_map/all_to_all | solution.py:519
  43.7 0.0 copy-done.4
  43.7 3.4 %solve.1 = (f32[50,64,128]{2,1,0:T(8,128)}, f32[64,128]{1,0:T(8,128)}, s32[1]{0:T(128)}) custom-call(f32[50]{0:T(128)} %weight.3, f32[128,128]{1,0:T(8,128)S(1)} %bitcast.5, f32[12,64,128]{2,1,0:T(8,128)S(1)} %get-tuple-element.145.basis, f32[50,64,128]{2,1,0:T(8,128)S(1)} %get-tuple-element.146.stepped, f32[64,128]{1,0:T(8,128)S(1)} %get-tuple-element.147.edges_y, ...), custom_call_target="tpu_custom_call" | custom-call | tf_op jit(solution)/shard_map/solve/pallas_call | solution.py:520
  47.0 0.0 copy-done.3
  47.0 0.0 copy-done.5
  47.1 0.6 %while.28 = (s32[]{:T(128)}, f32[50,64,128]{2,1,0:T(8,128)}, f32[64,128]{1,0:T(8,128)}, f32[50]{0:T(128)S(1)}, s32[64,128]{1,0:T(8,128)S(1)}, /*index=5*/f32[64,...) while((s32[]{:T(128)}, f32[50,64,128]{2,1,0:T(8,128)}, f32[64,128]{1,0:T(8,128)}, f32[50]{0:T(128)S(1)}, ...), condition=%region_9.0_spmd, body=%region_0.0_spmd | while | flops 1262598 | bytes 17688772 | solution.py:543
Async XLA Ops:
  0.6 43.0 %copy-start.4 = (s32[64,128]{1,0:T(8,128)S(1)}, s32[64,128]{1,0:T(8,128)}, u32[]{:S(2)}) copy-start(s32[64,128]{1,0:T(8,128)} %mask.3) | copy-start | bytes 98308
  8.1 7.2 %collective-permute-start.8 = (f32[248,128]{1,0:T(8,128)S(1)}, f32[248,128]{1,0:T(8,128)S(1)}, u32[]{:S(2)}, u32[]{:S(2)}) collective-permute-start(f32[248,128]{1,0:T(8,128)S(1)} %get-tuple-element.134.sent), channel_id=1, source_target_pairs={{0,1},{1,2},{2,3},{3,4},{4,5},{5,6},{6,7},{7,0},{8,9},{9,10},{10,1... | collective-permute-start | bytes 380936 | tf_op jit(solution)/shard_map/ppermute | solution.py:496
  11.2 4.2 %collective-permute-start.9 = (f32[184,128]{1,0:T(8,128)S(1)}, f32[184,128]{1,0:T(8,128)S(1)}, u32[]{:S(2)}, u32[]{:S(2)}) collective-permute-start(f32[184,128]{1,0:T(8,128)S(1)} %get-tuple-element.135), channel_id=1, source_target_pairs={{1,0},{2,1},{3,2},{4,3},{5,4},{6,5},{7,6},{0,7},{9,8},{10,9},{11,1... | collective-permute-start | bytes 282632 | tf_op jit(solution)/shard_map/ppermute | solution.py:497
  15.6 31.4 %copy-start.3 = (f32[64,128]{1,0:T(8,128)S(1)}, f32[64,128]{1,0:T(8,128)}, u32[]{:S(2)}) copy-start(f32[64,128]{1,0:T(8,128)} %column.1) | copy-start | bytes 98308
  15.7 31.4 %copy-start.5 = (f32[50]{0:T(128)S(1)}, f32[50]{0:T(128)}, u32[]{:S(2)}) copy-start(f32[50]{0:T(128)} %weight.3) | copy-start | bytes 604
  15.7 8.6 %collective-permute-start.10 = (f32[272,128]{1,0:T(8,128)S(1)}, f32[272,128]{1,0:T(8,128)S(1)}, u32[]{:S(2)}, u32[]{:S(2)}) collective-permute-start(f32[272,128]{1,0:T(8,128)S(1)} %get-tuple-element.140.down), channel_id=1, source_target_pairs={{0,8},{8,16},{16,24},{24,32},{32,40},{40,48},{48,56},{56,64},{64,7... | collective-permute-start | bytes 417800 | tf_op jit(solution)/shard_map/ppermute | solution.py:507
  16.9 5.8 %collective-permute-start.11 = (f32[216,128]{1,0:T(8,128)S(1)}, f32[216,128]{1,0:T(8,128)S(1)}, u32[]{:S(2)}, u32[]{:S(2)}) collective-permute-start(f32[216,128]{1,0:T(8,128)S(1)} %get-tuple-element.141.up), channel_id=1, source_target_pairs={{8,0},{16,8},{24,16},{32,24},{40,32},{48,40},{56,48},{64,56},{72,6... | collective-permute-start | bytes 331784 | tf_op jit(solution)/shard_map/ppermute | solution.py:508

commit v5 on v4

--- a/solution.py
+++ b/solution.py
@@ -78,12 +78,6 @@
         stepped[k] = value
         total = total + w * value
         kept[k] = half
-        edge_rows[0, pl.ds(k, 1), :] = here[NX - 1 :]
-        edge_rows[1, pl.ds(k, 1), :] = half[NX - 1 :]
-        edge_rows[2, pl.ds(k, 1), :] = half_u[NX - 1 :]
-        edge_rows[3, pl.ds(k, 1), :] = here[:1]
-        edge_rows[4, pl.ds(k, 1), :] = half[:1]
-        weights_out[pl.ds(k, 1), :] = jnp.full((1, NY), w, F32)
         return half_above, vertical, total
 
     def chunk(c, carry):
@@ -106,6 +100,13 @@
             at = 16 + 2 * k
             pair = (lane == at) | (lane == at + 1)
             half_v = vel_v[k].astype(F32) * (0.5 * scale[2, k])
+            half_u = vel_u[k].astype(F32) * (0.5 * scale[1, k])
+            edge_rows[0, pl.ds(k, 1), :] = lam[k, NX - 1 :]
+            edge_rows[1, pl.ds(k, 1), :] = kept[k, NX - 1 :]
+            edge_rows[2, pl.ds(k, 1), :] = half_u[NX - 1 :]
+            edge_rows[3, pl.ds(k, 1), :] = lam[k, :1]
+            edge_rows[4, pl.ds(k, 1), :] = kept[k, :1]
+            weights_out[pl.ds(k, 1), :] = jnp.full((1, NY), weight[k], F32)
             packs = (
                 jnp.where(pair, pltpu.roll(lam[k], at + 1, 1), packs[0]),
                 jnp.where(pair, pltpu.roll(kept[k], at + 1, 1), packs[1]),

time: 47.9 us -> 47.9 us (level)
  no operation moved by 1% of the time
where the time goes in v5:
time: 47.9 us; the launch traced here: 47.7 us
  blocking collectives  18 us (38%)
  Pallas kernels  12.5 us (26%)
  starting transfers between devices  8.12 us (17%)
  waiting for transfers between devices  7.66 us (16%)
  between operations  0.7 us (1%)
  loops' own time  0.64 us (1%)
    all_to_all x1, blocking collectives, on_device(): gathered = lax.all_to_all(dots, ('tx', 'ty'), 0, 0, tiled=True)  18 us
    pallas_call x1, Pallas kernels, on_device(): pl.pallas_call(interior_kernel, name='interior', in_specs=[smem] * 2 + [h...  7.5 us
    ppermute x1, waiting for transfers between devices, on_device(): from_north = lax.ppermute(short, 'ty', back)  4.17 us
    ppermute x1, starting transfers between devices, on_device(): from_down = lax.ppermute(up, 'tx', back)  3.8 us
    pallas_call x1, Pallas kernels, on_device(): pl.pallas_call(solve_kernel, name='solve', in_specs=[smem] + on_chip(6),...  3.37 us
    ppermute x1, starting transfers between devices, on_device(): from_south = lax.ppermute(sent, 'ty', onward)  3.04 us
    ppermute x1, waiting for transfers between devices, on_device(): from_down = lax.ppermute(up, 'tx', back)  1.98 us
    ppermute x1, waiting for transfers between devices, on_device(): from_up = lax.ppermute(down, 'tx', onward)  1.51 us
  transfers between devices with their start and end apart: 4, of which 3 were waited for; matrix products, arithmetic and copies ran while one was open for 0% of the time, Pallas kernels for 0%

profile of v5, /device:TPU:1, one launch (start us, length us, event | category | flops | bytes accessed | tf_op | source)
XLA Modules:
  0.0 47.7 jit_solution(5078486666598169617)
XLA Ops:
  0.6 0.0 copy-start.4
  0.6 7.5 %interior.1 = (f32[50,64,128]{2,1,0:T(8,128)S(1)}, f32[248,128]{1,0:T(8,128)S(1)}, f32[184,128]{1,0:T(8,128)S(1)}, f32[5,56,128]{2,1,0:T(8,128)S(1)}, f32[64,128...) custom-call(f32[3,50]{1,0:T(4,128)} %scale.1, f32[50]{0:T(128)} %weight.3, f32[50,64,128]{2,1,0:T(8,128)} %lam_hbm.1, ...), custom_call_target="tpu_custom_call" | custom-call | tf_op jit(solution)/shard_map/interior/pallas_call | solution.py:470
  8.1 3.0 %collective-permute-start.8 = (f32[248,128]{1,0:T(8,128)S(1)}, f32[248,128]{1,0:T(8,128)S(1)}, u32[]{:S(2)}, u32[]{:S(2)}) collective-permute-start(f32[248,128]{1,0:T(8,128)S(1)} %get-tuple-element.134.sent), channel_id=1, source_target_pairs={{0,1},{1,2},{2,3},{3,4},{4,5},{5,6},{6,7},{7,0},{8,9},{9,10},{10,1... | collective-permute-start | bytes 380936 | tf_op jit(solution)/shard_map/ppermute | solution.py:497
  11.2 0.0 collective-permute-start.9
  11.2 4.2 %collective-permute-done.9.from_north = f32[184,128]{1,0:T(8,128)S(1)} collective-permute-done((f32[184,128]{1,0:T(8,128)S(1)}, f32[184,128]{1,0:T(8,128)S(1)}, u32[]{:S(2)}, u32[]{:S(2)}) %collective-permute-start.9) | collective-permute-done | bytes 94240 | tf_op jit(solution)/shard_map/ppermute | solution.py:498
  15.4 0.0 collective-permute-done.8.from_south
  15.4 0.3 columns.1
  15.6 0.0 copy-start.3
  15.7 0.0 copy-start.5
  15.7 1.3 %collective-permute-start.10 = (f32[272,128]{1,0:T(8,128)S(1)}, f32[272,128]{1,0:T(8,128)S(1)}, u32[]{:S(2)}, u32[]{:S(2)}) collective-permute-start(f32[272,128]{1,0:T(8,128)S(1)} %get-tuple-element.140.down), channel_id=1, source_target_pairs={{0,8},{8,16},{16,24},{24,32},{32,40},{40,48},{48,56},{56,64},{64,7... | collective-permute-start | bytes 417800 | tf_op jit(solution)/shard_map/ppermute | solution.py:508
  17.0 3.8 %collective-permute-start.11 = (f32[216,128]{1,0:T(8,128)S(1)}, f32[216,128]{1,0:T(8,128)S(1)}, u32[]{:S(2)}, u32[]{:S(2)}) collective-permute-start(f32[216,128]{1,0:T(8,128)S(1)} %get-tuple-element.141.up), channel_id=1, source_target_pairs={{8,0},{16,8},{24,16},{32,24},{40,32},{48,40},{56,48},{64,56},{72,6... | collective-permute-start | bytes 331784 | tf_op jit(solution)/shard_map/ppermute | solution.py:509
  20.8 2.0 %collective-permute-done.11.from_down = f32[216,128]{1,0:T(8,128)S(1)} collective-permute-done((f32[216,128]{1,0:T(8,128)S(1)}, f32[216,128]{1,0:T(8,128)S(1)}, u32[]{:S(2)}, u32[]{:S(2)}) %collective-permute-start.11) | collective-permute-done | bytes 110624 | tf_op jit(solution)/shard_map/ppermute | solution.py:509
  22.7 1.5 %collective-permute-done.10.from_up = f32[272,128]{1,0:T(8,128)S(1)} collective-permute-done((f32[272,128]{1,0:T(8,128)S(1)}, f32[272,128]{1,0:T(8,128)S(1)}, u32[]{:S(2)}, u32[]{:S(2)}) %collective-permute-start.10) | collective-permute-done | bytes 139296 | tf_op jit(solution)/shard_map/ppermute | solution.py:508
  24.2 1.4 %basis.1 = (f32[12,64,128]{2,1,0:T(8,128)S(1)}, f32[128,128]{1,0:T(8,128)S(1)}, f32[112,128]{1,0:T(8,128)S(1)}, f32[64,128]{1,0:T(8,128)S(1)}) custom-call(f32[272,128]{1,0:T(8,128)S(1)} %collective-permute-done.10.from_up, f32[216,128]{1,0:T(8,128)S(1)} %collective-permute-done.11.from_down, f32[272,128]{1,0:T(8,128)S(1)} %get-tuple-element.140.down, ...), custom_call_target="tpu_custom_call" | custom-call | tf_op jit(solution)/shard_map/basis/pallas_call | solution.py:511
  25.6 18.0 %all_to_all.11 = f32[128,1,128]{2,1,0:T(1,128)S(1)} all-to-all(f32[128,1,128]{2,1,0:T(1,128)S(1)} %bitcast.6), channel_id=1, replica_groups=mesh['tx'=16,'ty'=8] {'tx','ty'}, dimensions={0} | all-to-all | bytes 131072 | tf_op jit(solution)/shard_map/all_to_all | solution.py:520
  43.7 0.0 copy-done.4
  43.7 3.4 %solve.1 = (f32[50,64,128]{2,1,0:T(8,128)}, f32[64,128]{1,0:T(8,128)}, s32[1]{0:T(128)}) custom-call(f32[50]{0:T(128)} %weight.3, f32[128,128]{1,0:T(8,128)S(1)} %bitcast.5, f32[12,64,128]{2,1,0:T(8,128)S(1)} %get-tuple-element.145.basis, f32[50,64,128]{2,1,0:T(8,128)S(1)} %get-tuple-element.146.stepped, f32[64,128]{1,0:T(8,128)S(1)} %get-tuple-element.147.edges_y, ...), custom_call_target="tpu_custom_call" | custom-call | tf_op jit(solution)/shard_map/solve/pallas_call | solution.py:521
  47.0 0.0 copy-done.3
  47.1 0.0 copy-done.5
  47.1 0.6 %while.28 = (s32[]{:T(128)}, f32[50,64,128]{2,1,0:T(8,128)}, f32[64,128]{1,0:T(8,128)}, f32[50]{0:T(128)S(1)}, s32[64,128]{1,0:T(8,128)S(1)}, /*index=5*/f32[64,...) while((s32[]{:T(128)}, f32[50,64,128]{2,1,0:T(8,128)}, f32[64,128]{1,0:T(8,128)}, f32[50]{0:T(128)S(1)}, ...), condition=%region_9.0_spmd, body=%region_0.0_spmd | while | flops 1262598 | bytes 17688772 | solution.py:544
Async XLA Ops:
  0.6 43.0 %copy-start.4 = (s32[64,128]{1,0:T(8,128)S(1)}, s32[64,128]{1,0:T(8,128)}, u32[]{:S(2)}) copy-start(s32[64,128]{1,0:T(8,128)} %mask.3) | copy-start | bytes 98308
  8.1 7.2 %collective-permute-start.8 = (f32[248,128]{1,0:T(8,128)S(1)}, f32[248,128]{1,0:T(8,128)S(1)}, u32[]{:S(2)}, u32[]{:S(2)}) collective-permute-start(f32[248,128]{1,0:T(8,128)S(1)} %get-tuple-element.134.sent), channel_id=1, source_target_pairs={{0,1},{1,2},{2,3},{3,4},{4,5},{5,6},{6,7},{7,0},{8,9},{9,10},{10,1... | collective-permute-start | bytes 380936 | tf_op jit(solution)/shard_map/ppermute | solution.py:497
  11.2 4.2 %collective-permute-start.9 = (f32[184,128]{1,0:T(8,128)S(1)}, f32[184,128]{1,0:T(8,128)S(1)}, u32[]{:S(2)}, u32[]{:S(2)}) collective-permute-start(f32[184,128]{1,0:T(8,128)S(1)} %get-tuple-element.135), channel_id=1, source_target_pairs={{1,0},{2,1},{3,2},{4,3},{5,4},{6,5},{7,6},{0,7},{9,8},{10,9},{11,1... | collective-permute-start | bytes 282632 | tf_op jit(solution)/shard_map/ppermute | solution.py:498
  15.6 31.4 %copy-start.3 = (f32[64,128]{1,0:T(8,128)S(1)}, f32[64,128]{1,0:T(8,128)}, u32[]{:S(2)}) copy-start(f32[64,128]{1,0:T(8,128)} %column.1) | copy-start | bytes 98308
  15.7 31.4 %copy-start.5 = (f32[50]{0:T(128)S(1)}, f32[50]{0:T(128)}, u32[]{:S(2)}) copy-start(f32[50]{0:T(128)} %weight.3) | copy-start | bytes 604
  15.7 8.6 %collective-permute-start.10 = (f32[272,128]{1,0:T(8,128)S(1)}, f32[272,128]{1,0:T(8,128)S(1)}, u32[]{:S(2)}, u32[]{:S(2)}) collective-permute-start(f32[272,128]{1,0:T(8,128)S(1)} %get-tuple-element.140.down), channel_id=1, source_target_pairs={{0,8},{8,16},{16,24},{24,32},{32,40},{40,48},{48,56},{56,64},{64,7... | collective-permute-start | bytes 417800 | tf_op jit(solution)/shard_map/ppermute | solution.py:508
  17.0 5.8 %collective-permute-start.11 = (f32[216,128]{1,0:T(8,128)S(1)}, f32[216,128]{1,0:T(8,128)S(1)}, u32[]{:S(2)}, u32[]{:S(2)}) collective-permute-start(f32[216,128]{1,0:T(8,128)S(1)} %get-tuple-element.141.up), channel_id=1, source_target_pairs={{8,0},{16,8},{24,16},{32,24},{40,32},{48,40},{56,48},{64,56},{72,6... | collective-permute-start | bytes 331784 | tf_op jit(solution)/shard_map/ppermute | solution.py:509
